TPU v7x, 128 devices: a whole 4x4x4 slice. The times are simulated.
128 devices in a mesh: dom: 32 (over y, x, core), near: 4 (over z).
Axes of the slice: x: 4, y: 4, z: 4, core: 2. Of those that a mesh axis runs over, the one named last changes fastest.
Arguments:
- start_block: float32 [131072, 128], P(('dom', 'near')), may hold values from -6 to 6
- near_tiles: float32 [6144, 128, 128], P(('dom', 'near')), may hold values from -0.09375 to 0.09375
- near_src: int32 [6144], P(('dom', 'near')), may hold values from 0 to 31, as said below
- near_mask: int32 [6144], P(('dom', 'near')), may hold values 0 or 1
- far_tiles: float32 [1024, 128, 128], P(('dom', 'near')), may hold values from -0.09375 to 0.09375
- far_src: int32 [1024], P(('dom', 'near')), may hold values from 0 to 31
- far_mask: int32 [1024], P(('dom', 'near')), may hold values 0 or 1
- bound_count: int32 [128], P(('dom', 'near')), may hold values from 1 to 128
Outputs:
- encodings: float32 [131072, 128], P(('dom', 'near'))
- rayleigh: float32 [128, 128], replicated
Inputs may be any that keep to these rules, and one draw needn't show every extreme that they name: `near_src`: each partition holds 48 consecutive slots; the slot at position j among them (j from 0) lies in tile row j // 6; the first slot of each tile row reads the partition's own tile of that row; every source tile from another partition of the group is one of that partition's first 4 tiles.
All inputs are finite; a program needn't handle non-finite values. No bound on the sum of `near_mask` or of `far_mask` on one device may be relied on, other than what follows from the above.
Results may differ from a plain program's by a relative error of at most 0.0003.
Values sent between devices are 32-bit elements; how exact they have to be, the bound alone decides.
No kernel may reach another device: no remote copies, remote signals or barrier semaphores. Data moves between devices by JAX's collectives and lax.ppermute only.
A program may use at most 64 MiB of HBM per device.

v0:
```python
from functools import partial

import jax
import jax.numpy as jnp
from jax import lax
from jax.experimental import pallas as pl
from jax.experimental.pallas import tpu as pltpu
from jax.sharding import PartitionSpec as P


TB = 128
NPER = 6
ROWS = 8
HEAD = 4
PANEL = 16
STEP = 2
CENTER = 1.3
HALF = 0.7
NODES = 131072
AXES = ("dom", "near")
NEAR_BUFFERS = 8 + 3 * HEAD
PARAMS = pltpu.CompilerParams(vmem_limit_bytes=8 << 20)


def pairs(first, second):
    out = []
    for y in range(4):
        for x in range(4):
            for c in range(2):
                for z in range(4):
                    dy, dx, dc, dz = second if c else first
                    there = (((y + dy) % 4) * 4 + (x + dx) % 4) * 2 + (c + dc) % 2
                    out.append((((y * 4 + x) * 2 + c) * 4 + z, there * 4 + (z + dz) % 4))
    return out


def shift(value, dy=0, dx=0, dc=0, dz=0):
    step = (dy, dx, dc, dz)
    return lax.ppermute(value, AXES, pairs(step, step))


def cross(value, along, stage):
    steps = ((0, along, 0, 0), (along, 0, 0, 0))
    return lax.ppermute(value, AXES, pairs(steps[stage], steps[1 - stage]))


def split(x):
    hi = x.astype(jnp.bfloat16)
    lo = (x - hi.astype(jnp.float32)).astype(jnp.bfloat16)
    return hi, lo


def wide(x):
    return jnp.concatenate(split(x), axis=1)


def tall(x):
    return jnp.concatenate(split(x), axis=0)


def fold(acc):
    return (acc[:TB, :TB] + acc[TB:, TB:]) + (acc[:TB, TB:] + acc[TB:, :TB])


def dot(a, b, dims):
    return lax.dot_general(a, b, (dims, ((), ())), preferred_element_type=jnp.float32)


def prep_kernel(near_src, near_mask, far_src, far_mask, here, near, far, own_ref, t_ref, table, near_v, far_v, sems):
    dom, z = here[0], here[1]
    core = dom & 1
    copies = [
        pltpu.make_async_copy(near.at[pl.ds(r * NPER, NPER)], near_v.at[pl.ds(r * NPER, NPER)], sems.at[r])
        for r in range(ROWS)
    ]
    copies.append(pltpu.make_async_copy(far, far_v, sems.at[ROWS]))
    for copy in copies:
        copy.start()

    def lookup(r, _):
        for s in range(NPER):
            if s < NPER - 1:
                source = near_src[r * NPER + s + 1]
                away = ((source >> 3) - z) & 3
                straight = jnp.where(core == 0, 3, 1)
                buffer = jnp.where(away == 2, 2, jnp.where(away == straight, 0, 1))
                halo = ROWS + buffer * HEAD + (source & 3)
                table[r * NPER + s] = jnp.where(away == 0, source & 7, halo)
            else:
                chip = far_src[r] >> 1
                dy = (0x78 >> 2 * (((chip >> 2) - (dom >> 3)) & 3)) & 3
                dx = (0x78 >> 2 * ((chip - (dom >> 1)) & 3)) & 3
                theirs = far_src[r] & 1
                inner = jnp.where(theirs == 0, dx, dy)
                outer = jnp.where(theirs == 0, dy, dx)
                piece = jnp.where(outer == 0, 0, jnp.where(outer == 3, 4, 8))
                swapped = jnp.where(outer == 2, inner * 8 + 5, (piece + inner) * 8 + 4)
                table[r * NPER + s] = jnp.where(theirs == core, inner * 8 + outer, swapped)

    lax.fori_loop(0, ROWS, lookup, None)
    table[ROWS * NPER] = core
    copies[ROWS].wait()

    def convert(r, _):
        pltpu.make_async_copy(near.at[pl.ds(r * NPER, NPER)], near_v.at[pl.ds(r * NPER, NPER)], sems.at[r]).wait()
        own_ref[r] = tall(near_v[r * NPER] * near_mask[r * NPER].astype(jnp.float32))
        for s in range(NPER):
            if s < NPER - 1:
                slot = r * NPER + s + 1
                tile = near_v[slot] * near_mask[slot].astype(jnp.float32)
            else:
                tile = far_v[r] * far_mask[r].astype(jnp.float32)
            t_ref[r, s // 2, :, pl.ds((s % 2) * TB, TB)] = tall(tile)

    lax.fori_loop(0, ROWS, convert, None)


def prepare(near_tiles, near_src, near_mask, far_tiles, far_src, far_mask):
    here = jnp.stack([lax.axis_index("dom"), lax.axis_index("near")]).astype(jnp.int32)
    in_hbm = lambda x: pltpu.with_memory_space_constraint(x, pltpu.MemorySpace.HBM)
    hbm, vmem, smem = (pl.BlockSpec(memory_space=getattr(pltpu.MemorySpace, m)) for m in ("HBM", "VMEM", "SMEM"))
    return pl.pallas_call(
        prep_kernel,
        in_specs=[smem] * 5 + [hbm] * 2,
        out_specs=[vmem, vmem, smem],
        out_shape=[
            jax.ShapeDtypeStruct((ROWS, 2 * TB, TB), jnp.bfloat16),
            jax.ShapeDtypeStruct((ROWS, NPER // 2, 2 * TB, 2 * TB), jnp.bfloat16),
            jax.ShapeDtypeStruct((ROWS * NPER + 1,), jnp.int32),
        ],
        scratch_shapes=[
            pltpu.VMEM((ROWS * NPER, TB, TB), jnp.float32),
            pltpu.VMEM((ROWS, TB, TB), jnp.float32),
            pltpu.SemaphoreType.DMA((ROWS + 1,)),
        ],
        compiler_params=PARAMS,
        name="prepare",
    )(*map(in_hbm, (near_src, near_mask, far_src, far_mask)), here, in_hbm(near_tiles), in_hbm(far_tiles))


def own_kernel(coefs, t_ref, head, tail, straight, crossed, *refs):
    own, times, back = coefs
    out, v_ref = refs[-2:]
    for half, part in enumerate((head, tail)):

        def row(t, _):
            here = tile_rows(t)
            r = half * HEAD + t
            tile = part[here, :]
            v_ref[r] = wide(tile)
            value = own * tile + times * fold(dot(t_ref[r], v_ref[r], ((1,), (0,))))
            if back:
                value = value - refs[half][here, :]
            out[tile_rows(r), :] = value

        lax.fori_loop(0, HEAD, row, None)

    def neighbour(t, _):
        for b, part in enumerate((straight, crossed)):
            v_ref[ROWS + b * HEAD + t] = wide(part[tile_rows(t), :])

    lax.fori_loop(0, HEAD, neighbour, None)


def tile_rows(t):
    return pl.ds(pl.multiple_of(t * TB, TB), TB)


def call(kernel, args, outs, scratch=(), scalars=0, aliases={}):
    vmem = pl.BlockSpec(memory_space=pltpu.MemorySpace.VMEM)
    smem = pl.BlockSpec(memory_space=pltpu.MemorySpace.SMEM)
    return pl.pallas_call(
        kernel,
        in_specs=[smem] * scalars + [vmem] * (len(args) - scalars),
        out_specs=[vmem] * len(outs),
        out_shape=outs,
        scratch_shapes=list(scratch),
        input_output_aliases=aliases,
        compiler_params=PARAMS,
    )(*args)


SOURCES = jax.ShapeDtypeStruct((NEAR_BUFFERS, TB, 2 * TB), jnp.bfloat16)
BLOCK = jax.ShapeDtypeStruct((ROWS * TB, TB), jnp.float32)
PART = jax.ShapeDtypeStruct((HEAD * TB, TB), jnp.float32)
SMALL = jax.ShapeDtypeStruct((TB, TB), jnp.float32)


def apply_own(coefs, tiles, state, prev, halo):
    args = [tiles[0], *state, *halo[:2], *(prev or ())]
    return call(partial(own_kernel, (*coefs, prev is not None)), args, [BLOCK, SOURCES])


def take_relayed(v_ref, relayed):
    def step(t, _):
        v_ref[ROWS + 2 * HEAD + t] = wide(relayed[tile_rows(t), :])

    lax.fori_loop(0, HEAD, step, None)


def finished_rows(times, index, t_ref, base, v_ref, far, out, store):
    def source(r, s):
        at = index[r * NPER + s]
        if s < NPER - 1:
            return v_ref[at]
        piece = at & 7
        here = tile_rows(at >> 3 & 3)
        tile = far[4][tile_rows(at >> 3), :]
        for b in (0, 1, 2, 3, 5):
            tile = jnp.where(piece == b, far[b][here, :], tile)
        return wide(tile)

    def half(h, _):
        for t in range(STEP):
            r = h * STEP + t
            acc = None
            for p in range(NPER // 2):
                rhs = jnp.concatenate([source(r, 2 * p), source(r, 2 * p + 1)], axis=0)
                part = dot(t_ref[r, p], rhs, ((1,), (0,)))
                acc = part if acc is None else acc + part
            out[tile_rows(r), :] = store(base[tile_rows(r), :] + times * fold(acc))

    lax.fori_loop(0, ROWS // STEP, half, None)


def rest_kernel(times, carries, index, bound, t_ref, base, *refs):
    far, relayed, _ = refs[:6], *refs[6:8]
    refs = list(refs[8:])
    parts = [refs.pop(0) for _ in range(3)] + [relayed] if carries == "take" else None
    v_ref, head, tail, edge = refs[:4]
    o_ref = refs[-1]
    take_relayed(v_ref, relayed)
    finished_rows(times, index, t_ref, base, v_ref, far, o_ref, lambda row: row)
    head[pl.ds(0, HEAD * TB), :] = o_ref[pl.ds(0, HEAD * TB), :]
    tail[...] = o_ref[pl.ds(HEAD * TB, HEAD * TB), :]
    rows = lax.broadcasted_iota(jnp.int32, (TB, TB), 0)
    edge[pl.ds(0, TB), :] = jnp.where(rows < bound[0], o_ref[pl.ds(0, TB), :], 0.0)
    if carries == "give":
        both = wide(o_ref[...])
        edge[pl.ds(TB, TB), :] = fold(dot(both, both, ((0,), (0,))))
    if carries == "pass":
        head[CARRY, :] = far[2][CARRY, :] + far[5][CARRY, :]
    if carries == "take":
        mine, straight, crossed, opposite = (part[CARRY, :] for part in parts)
        refs[4][...] = (mine + opposite) + (straight + crossed)


def last_kernel(times, index, t_ref, base, *refs):
    far, relayed, block, _, v_ref, out, o_ref = refs[:6], *refs[6:]
    take_relayed(v_ref, relayed)
    finished_rows(times, index, t_ref, base, v_ref, far, o_ref, wide)
    out[pl.ds(0, TB), :] = fold(dot(wide(block[...]), o_ref[...], ((0,), (0,))))
    out[pl.ds(TB, TB), :] = far[2][CARRY, :] + far[5][CARRY, :]


CARRY = pl.ds(HEAD * TB, TB)


def tiles_of(number):
    return jax.ShapeDtypeStruct((number * TB, TB), jnp.float32)


def apply_rest(times, carries, index, bound, tiles, base, v, relayed, far, parts):
    args = [index, bound, tiles[1], base, *far, relayed, v, *(parts if carries == "take" else ())]
    head = tiles_of(HEAD + 1) if carries == "pass" else PART
    outs = [SOURCES, head, PART, tiles_of(2) if carries == "give" else SMALL]
    outs += [SMALL] if carries == "take" else []
    scratch = [pltpu.VMEM((ROWS * TB, TB), jnp.float32)]
    _, head, tail, edge, *total = call(
        partial(rest_kernel, times, carries), args, outs, scratch, scalars=2, aliases={11: 0}
    )
    return [head, tail], edge, total


def apply_last(times, index, tiles, base, v, relayed, far, block):
    args = [index, tiles[1], base, *far, relayed, block, v]
    scratch = [pltpu.VMEM((ROWS * TB, 2 * TB), jnp.bfloat16)]
    return call(
        partial(last_kernel, times), args, [SOURCES, tiles_of(2)], scratch, scalars=1,
        aliases={len(args) - 1: 0},
    )[1]


def start_kernel(bound, block, head, tail, edge):
    head[...] = block[pl.ds(0, HEAD * TB), :]
    tail[...] = block[pl.ds(HEAD * TB, HEAD * TB), :]
    rows = lax.broadcasted_iota(jnp.int32, (TB, TB), 0)
    edge[...] = jnp.where(rows < bound[0], block[pl.ds(0, TB), :], 0.0)


def start(bound, block):
    vmem = pl.BlockSpec(memory_space=pltpu.MemorySpace.VMEM)
    head = jax.ShapeDtypeStruct((HEAD * TB, TB), jnp.float32)
    return pl.pallas_call(
        start_kernel,
        in_specs=[pl.BlockSpec(memory_space=pltpu.MemorySpace.SMEM), vmem],
        out_specs=[vmem] * 3,
        out_shape=[head, head, jax.ShapeDtypeStruct((TB, TB), jnp.float32)],
        compiler_params=PARAMS,
        name="begin",
    )(bound, block)


def pack_kernel(rows, carry, *refs):
    def step(t, _):
        for i, ref in enumerate(refs[:-1]):
            refs[-1][tile_rows(i * (rows // TB) + t), :] = ref[tile_rows(t), :]

    lax.fori_loop(0, rows // TB, step, None)
    at = rows * (len(refs) - 1)
    if carry:
        mine, straight, crossed, opposite = (ref[pl.ds(rows, TB), :] for ref in refs[:-1])
        refs[-1][pl.ds(at, TB), :] = (mine + opposite) + (straight + crossed)


def pack(rows, parts, carry=False):
    out = tiles_of(len(parts) * rows // TB + carry)
    return call(partial(pack_kernel, rows, carry), parts, [out])[0]


def sum_kernel(packed, one, three, two, out):
    rows = pl.ds(0, HEAD * TB)
    out[rows, :] = three[rows, :]
    out[CARRY, :] = (packed[CARRY, :] + two[CARRY, :]) + (one[CARRY, :] + three[CARRY, :])


def times_transpose(row, inv):
    return fold(dot(tall(row), inv, ((1,), (1,))))


def norm_kernel(head, tail, inverse, edge, out, both, o_ref):
    inv = tall(inverse[...])
    for half, part in enumerate((head, tail)):

        def step(h, _):
            for t in range(STEP):
                row = times_transpose(part[tile_rows(h * STEP + t), :], inv)
                where = tile_rows(half * HEAD + h * STEP + t)
                out[where, :] = row
                o_ref[where, :] = wide(row)

        lax.fori_loop(0, HEAD // STEP, step, None)
    both[pl.ds(0, TB), :] = edge[...]
    both[pl.ds(TB, TB), :] = fold(dot(o_ref[...], o_ref[...], ((0,), (0,))))


def normalise(state, inverse, edge):
    scratch = [pltpu.VMEM((ROWS * TB, 2 * TB), jnp.bfloat16)]
    return call(norm_kernel, [*state, inverse, edge], [BLOCK, tiles_of(2)], scratch)


def thirds(x):
    high = x.astype(jnp.bfloat16).astype(jnp.float32)
    rest = x - high
    middle = rest.astype(jnp.bfloat16).astype(jnp.float32)
    return high, middle, rest - middle


def factor(gram, aug):
    rows = lax.broadcasted_iota(jnp.int32, (TB, TB), 0)
    lanes = lax.broadcasted_iota(jnp.int32, (TB, TB), 1)
    aug[:, pl.ds(0, TB)] = gram
    aug[:, pl.ds(TB, TB)] = jnp.where(rows == lanes, 1.0, 0.0)
    sub = lax.broadcasted_iota(jnp.int32, (PANEL, TB), 0)
    lane = lax.broadcasted_iota(jnp.int32, (PANEL, TB), 1)
    below = lax.broadcasted_iota(jnp.int32, (TB, 2 * TB), 0)

    def step(number, _):
        at = pl.multiple_of(number * PANEL, PANEL)
        here = pl.ds(at, PANEL)
        left = aug[here, pl.ds(0, TB)]
        right = aug[here, pl.ds(TB, TB)]
        turned = pltpu.roll(left, TB - at, 1)
        columns = [jnp.broadcast_to(turned[:, k : k + 1], (PANEL, TB)) for k in range(PANEL)]
        for i in range(PANEL):
            times = jnp.where(sub > i, columns[i], 0.0) / columns[i][i : i + 1, :]
            for k in range(i + 1, PANEL):
                columns[k] = columns[k] - times * columns[k][i : i + 1, :]
            left = left - times * left[i : i + 1, :]
            right = right - times * right[i : i + 1, :]
        pivots = jnp.sum(jnp.where(lane == sub + at, left, 0.0), axis=1, keepdims=True)
        scale = lax.rsqrt(pivots)
        scale = scale * (1.5 - 0.5 * pivots * scale * scale)
        panel = jnp.concatenate([left * scale, right * scale], axis=1)
        high, middle, low = thirds(panel)
        a = [x[:, :TB] for x in (high, high, middle, high, middle, low)]
        b = [high, middle, high, low, middle, high]
        a = jnp.concatenate(a, axis=0).astype(jnp.bfloat16)
        b = jnp.concatenate(b, axis=0).astype(jnp.bfloat16)
        update = dot(a, b, ((0,), (0,)))
        aug[...] = jnp.where(below >= at + PANEL, aug[...] - update, aug[...])
        aug[here, :] = panel

    lax.fori_loop(0, TB // PANEL, step, None)
    return aug[:, pl.ds(TB, TB)]


def factor_kernel(gram, out, aug):
    out[...] = factor(gram[...] * (1.0 / NODES), aug)


def inverse_factor(gram):
    vmem = pl.BlockSpec(memory_space=pltpu.MemorySpace.VMEM)
    return pl.pallas_call(
        factor_kernel,
        in_specs=[vmem],
        out_specs=vmem,
        out_shape=jax.ShapeDtypeStruct((TB, TB), jnp.float32),
        scratch_shapes=[pltpu.VMEM((TB, 2 * TB), jnp.float32)],
        compiler_params=PARAMS,
        name="factor",
    )(gram)


def encode_kernel(block, inverse, out):
    inv = tall(inverse[...])

    def step(h, _):
        for t in range(HEAD):
            where = tile_rows(h * HEAD + t)
            out[where, :] = times_transpose(block[where, :], inv)

    lax.fori_loop(0, ROWS // HEAD, step, None)


def rayleigh_kernel(projection, first, second, out):
    inv = tall(second[...])
    right = times_transpose(projection[...] * (1.0 / NODES), tall(first[...]))
    out[...] = times_transpose(fold(dot(inv, wide(right), ((1,), (0,)))), inv)


def relay(value, along):
    return lax.ppermute(value, AXES, pairs((0, 0, 0, along), (0, 0, 0, -along)))


def exchange(head, edge, carry):
    straight = relay(head, 1)
    first = {i: cross(edge, i, 0) for i in (2, 1, 3)}
    crossed = relay(head, -1)
    forwarded = relay(straight, 1)
    packed = pack(TB, [edge, first[1], first[3], first[2]], carry)
    second = {i: cross(packed, i, 1) for i in (2, 1, 3)}
    early = pack(HEAD * TB, [packed, second[2], second[1]])
    late = second[3]
    if carry:
        (late,) = call(sum_kernel, [packed, second[1], second[3], second[2]], [tiles_of(HEAD + 1)])
    theirs = [shift(early, dc=1), shift(late, dc=1)]
    return [straight, crossed, forwarded], [packed, second[1], late, second[2]] + theirs


def ring_sum(value, axis):
    two, one, three = (shift(value, **{"d" + axis: step}) for step in (2, 1, 3))
    return (value + two) + (one + three)


def steps(start_block, near_tiles, near_src, near_mask, far_tiles, far_src, far_mask, bound_count):
    *tiles, index = prepare(near_tiles, near_src, near_mask, far_tiles, far_src, far_mask)
    first = ((1.0 - CENTER) / HALF, -1.0 / HALF)
    later = (2.0 * first[0], 2.0 * first[1])

    *state, edge = start(bound_count, start_block)
    plan = (
        [("step", first, False), ("step", later, True), ("gram", later, True)]
        + [("step", first, False), ("step", later, True), ("step", later, True)]
        + [("last", (1.0, -1.0), False)]
    )
    carries = {3: "give", 4: "pass", 5: "take"}
    before = None
    for number, (kind, coefs, back) in enumerate(plan, 1):
        if kind == "last":
            block, edge = normalise(state, inverse, edge)
        halo, far = exchange(state[0], edge, number in (4, 7))
        base, v = apply_own(coefs, tiles, state, before if back else None, halo)
        if number == 6:
            inverse = inverse_factor(gram)
        if kind == "last":
            value = apply_last(coefs[1], index, tiles, base, v, halo[2], far, block)
        else:
            parts = [state[0], *halo[:2]]
            before = state
            state, edge, total = apply_rest(
                coefs[1], carries.get(number), index, bound_count, tiles, base, v, halo[2], far, parts
            )
            if total:
                (gram,) = total
    value = ring_sum(value, "z")
    second = inverse_factor(value[TB:])
    (encodings,) = call(encode_kernel, [block, second], [BLOCK])
    projection = value[:TB]
    projection = projection + shift(projection, dc=1)
    projection = ring_sum(ring_sum(projection, "x"), "y")
    (rayleigh,) = call(rayleigh_kernel, [projection, inverse, second], [SMALL])
    return encodings, rayleigh


def solution(mesh):
    rows = P(AXES)
    return jax.shard_map(
        steps,
        mesh=mesh,
        in_specs=(rows,) * 8,
        out_specs=(rows, P()),
        check_vma=False,
    )
```

profile of v0, /device:TPU:1, one launch (start us, length us, event | category | flops | bytes accessed | tf_op | source)
XLA Modules:
  0.0 324.6 jit_solution(15680209470814101606)
XLA Ops:
  2.4 3.8 %collective-permute-start.4 = (f32[128,128]{1,0:T(8,128)S(1)}, f32[128,128]{1,0:T(8,128)S(1)}, u32[]{:S(2)}, u32[]{:S(2)}) collective-permute-start(f32[128,128]{1,0:T(8,128)S(1)} %get-tuple-element.50.refs_0_), channel_id=1, source_target_pairs={{0,16},{1,17},{2,18},{3,19},{4,68},{5,69},{6,70},{7,71},{8,24},{9,... | collective-permute-start | bytes 196616 | tf_op jit(solution)/shard_map/ppermute | solution.py:44
  14.4 4.0 %collective-permute-done.7.refs_1_.refs_3_ = f32[512,128]{1,0:T(8,128)S(1)} collective-permute-done((f32[512,128]{1,0:T(8,128)S(1)}, f32[512,128]{1,0:T(8,128)S(1)}, u32[]{:S(2)}, u32[]{:S(2)}) %collective-permute-start.7) | collective-permute-done | bytes 262176 | tf_op jit(solution)/shard_map/ppermute | solution.py:44
  24.6 3.8 %collective-permute-start = (f32[512,128]{1,0:T(8,128)S(1)}, f32[512,128]{1,0:T(8,128)}, u32[]{:S(2)}, u32[]{:S(2)}) collective-permute-start(f32[512,128]{1,0:T(8,128)S(1)} %get-tuple-element.47.head.refs_0_), channel_id=1, source_target_pairs={{0,1},{1,2},{2,3},{3,0},{4,7},{5,4},{6,5},{7,6},{8,9},{9,10},{10,1... | collective-permute-start | bytes 786440 | tf_op jit(solution)/shard_map/ppermute | solution.py:433
  28.4 5.0 %collective-permute-done.straight = f32[512,128]{1,0:T(8,128)} collective-permute-done((f32[512,128]{1,0:T(8,128)S(1)}, f32[512,128]{1,0:T(8,128)}, u32[]{:S(2)}, u32[]{:S(2)}) %collective-permute-start) | collective-permute-done | bytes 262176 | tf_op jit(solution)/shard_map/ppermute | solution.py:433
  37.0 4.0 %prepare.1 = (bf16[8,256,128]{2,1,0:T(8,128)(2,1)S(1)}, bf16[8,3,256,256]{3,2,1,0:T(8,128)(2,1)S(1)}, s32[49]{0:T(128)S(1)}) custom-call(s32[48]{0:T(128)} %near_src.1, s32[48]{0:T(128)} %near_mask.1, s32[8]{0:T(128)} %far_src.1, s32[8]{0:T(128)} %far_mask.1, s32[2]{0:T(128)S(1)} %pad_add_fusion.here, f32[48,128,128]{2,1,0:T(8,128)} %near.1, f32[8,128,128]{2,1,0:T(8,128)} %far.1), custom_call_target="tpu_custom_call" | custom-call | tf_op jit(solution)/shard_map/prepare/pallas_call | solution.py:122
  54.9 6.8 %collective-permute-done.18.refs_1_.refs_3_ = f32[512,128]{1,0:T(8,128)S(1)} collective-permute-done((f32[512,128]{1,0:T(8,128)S(1)}, f32[512,128]{1,0:T(8,128)S(1)}, u32[]{:S(2)}, u32[]{:S(2)}) %collective-permute-start.18) | collective-permute-done | bytes 262176 | tf_op jit(solution)/shard_map/ppermute | solution.py:44
  67.3 5.4 %collective-permute-done.11.straight = f32[512,128]{1,0:T(8,128)S(1)} collective-permute-done((f32[512,128]{1,0:T(8,128)S(1)}, f32[512,128]{1,0:T(8,128)S(1)}, u32[]{:S(2)}, u32[]{:S(2)}) %collective-permute-start.11) | collective-permute-done | bytes 262176 | tf_op jit(solution)/shard_map/ppermute | solution.py:433
  87.0 7.3 %collective-permute-done.29.refs_1_.refs_3_ = f32[512,128]{1,0:T(8,128)S(1)} collective-permute-done((f32[512,128]{1,0:T(8,128)S(1)}, f32[512,128]{1,0:T(8,128)S(1)}, u32[]{:S(2)}, u32[]{:S(2)}) %collective-permute-start.29) | collective-permute-done | bytes 262176 | tf_op jit(solution)/shard_map/ppermute | solution.py:44
  96.9 9.8 %collective-permute-start.30 = (f32[1536,128]{1,0:T(8,128)S(1)}, f32[1536,128]{1,0:T(8,128)S(1)}, u32[]{:S(2)}, u32[]{:S(2)}) collective-permute-start(f32[1536,128]{1,0:T(8,128)S(1)} %shard_map.105), channel_id=1, source_target_pairs={{0,4},{1,5},{2,6},{3,7},{4,0},{5,1},{6,2},{7,3},{8,12},{9,13},{10,... | collective-permute-start | bytes 2359304 | tf_op jit(solution)/shard_map/ppermute | solution.py:39
  108.1 5.6 %collective-permute-done.22.straight = f32[512,128]{1,0:T(8,128)S(1)} collective-permute-done((f32[512,128]{1,0:T(8,128)S(1)}, f32[512,128]{1,0:T(8,128)S(1)}, u32[]{:S(2)}, u32[]{:S(2)}) %collective-permute-start.22) | collective-permute-done | bytes 262176 | tf_op jit(solution)/shard_map/ppermute | solution.py:433
  128.6 9.0 %collective-permute-done.40.two.refs_1_.refs_3_ = f32[640,128]{1,0:T(8,128)S(1)} collective-permute-done((f32[640,128]{1,0:T(8,128)S(1)}, f32[640,128]{1,0:T(8,128)S(1)}, u32[]{:S(2)}, u32[]{:S(2)}) %collective-permute-start.40) | collective-permute-done | bytes 327712 | tf_op jit(solution)/shard_map/ppermute | solution.py:44
  141.1 10.8 %collective-permute-start.41 = (f32[1536,128]{1,0:T(8,128)S(1)}, f32[1536,128]{1,0:T(8,128)S(1)}, u32[]{:S(2)}, u32[]{:S(2)}) collective-permute-start(f32[1536,128]{1,0:T(8,128)S(1)} %shard_map.110), channel_id=1, source_target_pairs={{0,4},{1,5},{2,6},{3,7},{4,0},{5,1},{6,2},{7,3},{8,12},{9,13},{10,... | collective-permute-start | bytes 2359304 | tf_op jit(solution)/shard_map/ppermute | solution.py:39
  151.9 6.2 %collective-permute-done.39.three = f32[640,128]{1,0:T(8,128)S(1)} collective-permute-done((f32[640,128]{1,0:T(8,128)S(1)}, f32[640,128]{1,0:T(8,128)S(1)}, u32[]{:S(2)}, u32[]{:S(2)}) %collective-permute-start.39) | collective-permute-done | bytes 327712 | tf_op jit(solution)/shard_map/ppermute | solution.py:44
  161.9 5.4 %collective-permute-done.34.crossed = f32[512,128]{1,0:T(8,128)S(1)} collective-permute-done((f32[512,128]{1,0:T(8,128)S(1)}, f32[512,128]{1,0:T(8,128)S(1)}, u32[]{:S(2)}, u32[]{:S(2)}) %collective-permute-start.34) | collective-permute-done | bytes 262176 | tf_op jit(solution)/shard_map/ppermute | solution.py:433
  178.1 7.0 %collective-permute-done.51.refs_1_.refs_3_ = f32[512,128]{1,0:T(8,128)S(1)} collective-permute-done((f32[512,128]{1,0:T(8,128)S(1)}, f32[512,128]{1,0:T(8,128)S(1)}, u32[]{:S(2)}, u32[]{:S(2)}) %collective-permute-start.51) | collective-permute-done | bytes 262176 | tf_op jit(solution)/shard_map/ppermute | solution.py:44
  192.3 6.5 %collective-permute-done.44.straight.refs_9_ = f32[640,128]{1,0:T(8,128)S(1)} collective-permute-done((f32[640,128]{1,0:T(8,128)S(1)}, f32[640,128]{1,0:T(8,128)S(1)}, u32[]{:S(2)}, u32[]{:S(2)}) %collective-permute-start.44) | collective-permute-done | bytes 327712 | tf_op jit(solution)/shard_map/ppermute | solution.py:433
  213.5 7.1 %collective-permute-done.62.refs_1_.refs_3_ = f32[512,128]{1,0:T(8,128)S(1)} collective-permute-done((f32[512,128]{1,0:T(8,128)S(1)}, f32[512,128]{1,0:T(8,128)S(1)}, u32[]{:S(2)}, u32[]{:S(2)}) %collective-permute-start.62) | collective-permute-done | bytes 262176 | tf_op jit(solution)/shard_map/ppermute | solution.py:44
  223.3 10.0 %collective-permute-start.63 = (f32[1536,128]{1,0:T(8,128)S(1)}, f32[1536,128]{1,0:T(8,128)S(1)}, u32[]{:S(2)}, u32[]{:S(2)}) collective-permute-start(f32[1536,128]{1,0:T(8,128)S(1)} %shard_map.118), channel_id=1, source_target_pairs={{0,4},{1,5},{2,6},{3,7},{4,0},{5,1},{6,2},{7,3},{8,12},{9,13},{10,... | collective-permute-start | bytes 2359304 | tf_op jit(solution)/shard_map/ppermute | solution.py:39
  234.7 5.6 %collective-permute-done.55.straight = f32[512,128]{1,0:T(8,128)S(1)} collective-permute-done((f32[512,128]{1,0:T(8,128)S(1)}, f32[512,128]{1,0:T(8,128)S(1)}, u32[]{:S(2)}, u32[]{:S(2)}) %collective-permute-start.55) | collective-permute-done | bytes 262176 | tf_op jit(solution)/shard_map/ppermute | solution.py:433
  243.2 5.1 %factor.2.inverse.first = f32[128,128]{1,0:T(8,128)S(1)} custom-call(f32[128,128]{1,0:T(8,128)S(1)} %get-tuple-element.79.gram), custom_call_target="tpu_custom_call" | custom-call | tf_op jit(solution)/shard_map/factor/pallas_call | solution.py:404
  260.8 7.6 %collective-permute-done.73.two.refs_1_.refs_3_ = f32[640,128]{1,0:T(8,128)S(1)} collective-permute-done((f32[640,128]{1,0:T(8,128)S(1)}, f32[640,128]{1,0:T(8,128)S(1)}, u32[]{:S(2)}, u32[]{:S(2)}) %collective-permute-start.73) | collective-permute-done | bytes 327712 | tf_op jit(solution)/shard_map/ppermute | solution.py:44
  298.6 4.9 %collective-permute-done.78 = f32[256,128]{1,0:T(8,128)S(1)} collective-permute-done((f32[256,128]{1,0:T(8,128)S(1)}, f32[256,128]{1,0:T(8,128)S(1)}, u32[]{:S(2)}, u32[]{:S(2)}) %collective-permute-start.78) | collective-permute-done | bytes 131104 | tf_op jit(solution)/shard_map/ppermute | solution.py:39
  310.8 3.8 %collective-permute-done.82 = f32[128,128]{1,0:T(8,128)S(1)} collective-permute-done((f32[128,128]{1,0:T(8,128)S(1)}, f32[128,128]{1,0:T(8,128)S(1)}, u32[]{:S(2)}, u32[]{:S(2)}) %collective-permute-start.82) | collective-permute-done | bytes 65568 | tf_op jit(solution)/shard_map/ppermute | solution.py:39
  316.9 5.1 %factor.3.inverse.second = f32[128,128]{1,0:T(8,128)S(1)} custom-call(f32[128,128]{1,0:T(8,128)S(1)} %get-tuple-element.87.gram), custom_call_target="tpu_custom_call" | custom-call | tf_op jit(solution)/shard_map/factor/pallas_call | solution.py:404
  (195 shorter events, 173.4 us)
Async XLA Ops:
  21.2 22.4 %collective-permute-start.8 = (f32[1536,128]{1,0:T(8,128)S(1)}, f32[1536,128]{1,0:T(8,128)S(1)}, u32[]{:S(2)}, u32[]{:S(2)}) collective-permute-start(f32[1536,128]{1,0:T(8,128)S(1)} %shard_map.97), channel_id=1, source_target_pairs={{0,4},{1,5},{2,6},{3,7},{4,0},{5,1},{6,2},{7,3},{8,12},{9,13},{10,... | collective-permute-start | bytes 2359304 | tf_op jit(solution)/shard_map/ppermute | solution.py:39
  28.4 12.7 %collective-permute-start.1 = (f32[512,128]{1,0:T(8,128)S(1)}, f32[512,128]{1,0:T(8,128)}, u32[]{:S(2)}, u32[]{:S(2)}) collective-permute-start(f32[512,128]{1,0:T(8,128)S(1)} %get-tuple-element.47.head.refs_0_), channel_id=1, source_target_pairs={{0,3},{1,0},{2,1},{3,2},{4,5},{5,6},{6,7},{7,4},{8,11},{9,8},{10,9... | collective-permute-start | bytes 786440 | tf_op jit(solution)/shard_map/ppermute | solution.py:433
  33.4 10.2 %collective-permute-start.10 = (f32[512,128]{1,0:T(8,128)}, f32[512,128]{1,0:T(8,128)S(1)}, u32[]{:S(2)}, u32[]{:S(2)}) collective-permute-start(f32[512,128]{1,0:T(8,128)} %collective-permute-done.straight), channel_id=1, source_target_pairs={{0,1},{1,2},{2,3},{3,0},{4,7},{5,4},{6,5},{7,6},{8,9},{9,10},{10,1... | collective-permute-start | bytes 786440 | tf_op jit(solution)/shard_map/ppermute | solution.py:433
  54.7 9.6 %collective-permute-start.16 = (f32[512,128]{1,0:T(8,128)S(1)}, f32[512,128]{1,0:T(8,128)S(1)}, u32[]{:S(2)}, u32[]{:S(2)}) collective-permute-start(f32[512,128]{1,0:T(8,128)S(1)} %shard_map.100.refs_0_), channel_id=1, source_target_pairs={{0,32},{1,33},{2,34},{3,35},{4,12},{5,13},{6,14},{7,15},{8,40},{9,... | collective-permute-start | bytes 786440 | tf_op jit(solution)/shard_map/ppermute | solution.py:44
  64.3 13.6 %collective-permute-start.19 = (f32[1536,128]{1,0:T(8,128)S(1)}, f32[1536,128]{1,0:T(8,128)S(1)}, u32[]{:S(2)}, u32[]{:S(2)}) collective-permute-start(f32[1536,128]{1,0:T(8,128)S(1)} %shard_map.101), channel_id=1, source_target_pairs={{0,4},{1,5},{2,6},{3,7},{4,0},{5,1},{6,2},{7,3},{8,12},{9,13},{10,... | collective-permute-start | bytes 2359304 | tf_op jit(solution)/shard_map/ppermute | solution.py:39
  65.9 9.9 %collective-permute-start.12 = (f32[512,128]{1,0:T(8,128)S(1)}, f32[512,128]{1,0:T(8,128)S(1)}, u32[]{:S(2)}, u32[]{:S(2)}) collective-permute-start(f32[512,128]{1,0:T(8,128)S(1)} %get-tuple-element.52.head.refs_0_), channel_id=1, source_target_pairs={{0,3},{1,0},{2,1},{3,2},{4,5},{5,6},{6,7},{7,4},{8,11},{9,8},{10,9... | collective-permute-start | bytes 786440 | tf_op jit(solution)/shard_map/ppermute | solution.py:433
  86.1 10.7 %collective-permute-start.27 = (f32[512,128]{1,0:T(8,128)S(1)}, f32[512,128]{1,0:T(8,128)S(1)}, u32[]{:S(2)}, u32[]{:S(2)}) collective-permute-start(f32[512,128]{1,0:T(8,128)S(1)} %shard_map.104.refs_0_), channel_id=1, source_target_pairs={{0,32},{1,33},{2,34},{3,35},{4,12},{5,13},{6,14},{7,15},{8,40},{9,... | collective-permute-start | bytes 786440 | tf_op jit(solution)/shard_map/ppermute | solution.py:44
  96.9 22.1 %collective-permute-start.30 = (f32[1536,128]{1,0:T(8,128)S(1)}, f32[1536,128]{1,0:T(8,128)S(1)}, u32[]{:S(2)}, u32[]{:S(2)}) collective-permute-start(f32[1536,128]{1,0:T(8,128)S(1)} %shard_map.105), channel_id=1, source_target_pairs={{0,4},{1,5},{2,6},{3,7},{4,0},{5,1},{6,2},{7,3},{8,12},{9,13},{10,... | collective-permute-start | bytes 2359304 | tf_op jit(solution)/shard_map/ppermute | solution.py:39
  106.7 9.9 %collective-permute-start.23 = (f32[512,128]{1,0:T(8,128)S(1)}, f32[512,128]{1,0:T(8,128)S(1)}, u32[]{:S(2)}, u32[]{:S(2)}) collective-permute-start(f32[512,128]{1,0:T(8,128)S(1)} %get-tuple-element.57.head), channel_id=1, source_target_pairs={{0,3},{1,0},{2,1},{3,2},{4,5},{5,6},{6,7},{7,4},{8,11},{9,8},{10,9... | collective-permute-start | bytes 786440 | tf_op jit(solution)/shard_map/ppermute | solution.py:433
  128.5 12.6 %collective-permute-start.38 = (f32[640,128]{1,0:T(8,128)S(1)}, f32[640,128]{1,0:T(8,128)S(1)}, u32[]{:S(2)}, u32[]{:S(2)}) collective-permute-start(f32[640,128]{1,0:T(8,128)S(1)} %shard_map.108.packed.refs_0_), channel_id=1, source_target_pairs={{0,32},{1,33},{2,34},{3,35},{4,12},{5,13},{6,14},{7,15},{8,40},{9,... | collective-permute-start | bytes 983048 | tf_op jit(solution)/shard_map/ppermute | solution.py:44
  141.1 27.8 %collective-permute-start.41 = (f32[1536,128]{1,0:T(8,128)S(1)}, f32[1536,128]{1,0:T(8,128)S(1)}, u32[]{:S(2)}, u32[]{:S(2)}) collective-permute-start(f32[1536,128]{1,0:T(8,128)S(1)} %shard_map.110), channel_id=1, source_target_pairs={{0,4},{1,5},{2,6},{3,7},{4,0},{5,1},{6,2},{7,3},{8,12},{9,13},{10,... | collective-permute-start | bytes 2359304 | tf_op jit(solution)/shard_map/ppermute | solution.py:39
  158.2 10.7 %collective-permute-start.42 = (f32[640,128]{1,0:T(8,128)S(1)}, f32[640,128]{1,0:T(8,128)S(1)}, u32[]{:S(2)}, u32[]{:S(2)}) collective-permute-start(f32[640,128]{1,0:T(8,128)S(1)} %shard_map.109.refs_2_), channel_id=1, source_target_pairs={{0,4},{1,5},{2,6},{3,7},{4,0},{5,1},{6,2},{7,3},{8,12},{9,13},{10,... | collective-permute-start | bytes 983048 | tf_op jit(solution)/shard_map/ppermute | solution.py:39
  159.2 9.6 %collective-permute-start.43 = (f32[512,128]{1,0:T(8,128)S(1)}, f32[512,128]{1,0:T(8,128)S(1)}, u32[]{:S(2)}, u32[]{:S(2)}) collective-permute-start(f32[512,128]{1,0:T(8,128)S(1)} %collective-permute-done.33.straight), channel_id=1, source_target_pairs={{0,1},{1,2},{2,3},{3,0},{4,7},{5,4},{6,5},{7,6},{8,9},{9,10},{10,1... | collective-permute-start | bytes 786440 | tf_op jit(solution)/shard_map/ppermute | solution.py:433
  178.0 9.6 %collective-permute-start.49 = (f32[512,128]{1,0:T(8,128)S(1)}, f32[512,128]{1,0:T(8,128)S(1)}, u32[]{:S(2)}, u32[]{:S(2)}) collective-permute-start(f32[512,128]{1,0:T(8,128)S(1)} %shard_map.113.refs_0_), channel_id=1, source_target_pairs={{0,32},{1,33},{2,34},{3,35},{4,12},{5,13},{6,14},{7,15},{8,40},{9,... | collective-permute-start | bytes 786440 | tf_op jit(solution)/shard_map/ppermute | solution.py:44
  187.7 17.1 %collective-permute-start.52 = (f32[1536,128]{1,0:T(8,128)S(1)}, f32[1536,128]{1,0:T(8,128)S(1)}, u32[]{:S(2)}, u32[]{:S(2)}) collective-permute-start(f32[1536,128]{1,0:T(8,128)S(1)} %shard_map.114), channel_id=1, source_target_pairs={{0,4},{1,5},{2,6},{3,7},{4,0},{5,1},{6,2},{7,3},{8,12},{9,13},{10,... | collective-permute-start | bytes 2359304 | tf_op jit(solution)/shard_map/ppermute | solution.py:39
  190.8 11.3 %collective-permute-start.45 = (f32[640,128]{1,0:T(8,128)S(1)}, f32[640,128]{1,0:T(8,128)S(1)}, u32[]{:S(2)}, u32[]{:S(2)}) collective-permute-start(f32[640,128]{1,0:T(8,128)S(1)} %get-tuple-element.67.head.refs_8_.refs_0_), channel_id=1, source_target_pairs={{0,3},{1,0},{2,1},{3,2},{4,5},{5,6},{6,7},{7,4},{8,11},{9,8},{10,9... | collective-permute-start | bytes 983048 | tf_op jit(solution)/shard_map/ppermute | solution.py:433
  212.5 10.7 %collective-permute-start.60 = (f32[512,128]{1,0:T(8,128)S(1)}, f32[512,128]{1,0:T(8,128)S(1)}, u32[]{:S(2)}, u32[]{:S(2)}) collective-permute-start(f32[512,128]{1,0:T(8,128)S(1)} %shard_map.117.refs_0_), channel_id=1, source_target_pairs={{0,32},{1,33},{2,34},{3,35},{4,12},{5,13},{6,14},{7,15},{8,40},{9,... | collective-permute-start | bytes 786440 | tf_op jit(solution)/shard_map/ppermute | solution.py:44
  223.3 26.6 %collective-permute-start.63 = (f32[1536,128]{1,0:T(8,128)S(1)}, f32[1536,128]{1,0:T(8,128)S(1)}, u32[]{:S(2)}, u32[]{:S(2)}) collective-permute-start(f32[1536,128]{1,0:T(8,128)S(1)} %shard_map.118), channel_id=1, source_target_pairs={{0,4},{1,5},{2,6},{3,7},{4,0},{5,1},{6,2},{7,3},{8,12},{9,13},{10,... | collective-permute-start | bytes 2359304 | tf_op jit(solution)/shard_map/ppermute | solution.py:39
  233.3 15.1 %collective-permute-start.56 = (f32[512,128]{1,0:T(8,128)S(1)}, f32[512,128]{1,0:T(8,128)S(1)}, u32[]{:S(2)}, u32[]{:S(2)}) collective-permute-start(f32[512,128]{1,0:T(8,128)S(1)} %get-tuple-element.72.head), channel_id=1, source_target_pairs={{0,3},{1,0},{2,1},{3,2},{4,5},{5,6},{6,7},{7,4},{8,11},{9,8},{10,9... | collective-permute-start | bytes 786440 | tf_op jit(solution)/shard_map/ppermute | solution.py:433
  240.3 9.5 %collective-permute-start.65 = (f32[512,128]{1,0:T(8,128)S(1)}, f32[512,128]{1,0:T(8,128)S(1)}, u32[]{:S(2)}, u32[]{:S(2)}) collective-permute-start(f32[512,128]{1,0:T(8,128)S(1)} %collective-permute-done.55.straight), channel_id=1, source_target_pairs={{0,1},{1,2},{2,3},{3,0},{4,7},{5,4},{6,5},{7,6},{8,9},{9,10},{10,1... | collective-permute-start | bytes 786440 | tf_op jit(solution)/shard_map/ppermute | solution.py:433
  240.4 9.5 %collective-permute-start.64 = (f32[512,128]{1,0:T(8,128)S(1)}, f32[512,128]{1,0:T(8,128)S(1)}, u32[]{:S(2)}, u32[]{:S(2)}) collective-permute-start(f32[512,128]{1,0:T(8,128)S(1)} %collective-permute-done.61.refs_2_), channel_id=1, source_target_pairs={{0,4},{1,5},{2,6},{3,7},{4,0},{5,1},{6,2},{7,3},{8,12},{9,13},{10,... | collective-permute-start | bytes 786440 | tf_op jit(solution)/shard_map/ppermute | solution.py:39
  260.7 11.0 %collective-permute-start.71 = (f32[640,128]{1,0:T(8,128)S(1)}, f32[640,128]{1,0:T(8,128)S(1)}, u32[]{:S(2)}, u32[]{:S(2)}) collective-permute-start(f32[640,128]{1,0:T(8,128)S(1)} %shard_map.122.packed.refs_0_), channel_id=1, source_target_pairs={{0,32},{1,33},{2,34},{3,35},{4,12},{5,13},{6,14},{7,15},{8,40},{9,... | collective-permute-start | bytes 983048 | tf_op jit(solution)/shard_map/ppermute | solution.py:44
  271.7 19.0 %collective-permute-start.74 = (f32[1536,128]{1,0:T(8,128)S(1)}, f32[1536,128]{1,0:T(8,128)S(1)}, u32[]{:S(2)}, u32[]{:S(2)}) collective-permute-start(f32[1536,128]{1,0:T(8,128)S(1)} %shard_map.124), channel_id=1, source_target_pairs={{0,4},{1,5},{2,6},{3,7},{4,0},{5,1},{6,2},{7,3},{8,12},{9,13},{10,... | collective-permute-start | bytes 2359304 | tf_op jit(solution)/shard_map/ppermute | solution.py:39
  280.9 9.8 %collective-permute-start.75 = (f32[640,128]{1,0:T(8,128)S(1)}, f32[640,128]{1,0:T(8,128)S(1)}, u32[]{:S(2)}, u32[]{:S(2)}) collective-permute-start(f32[640,128]{1,0:T(8,128)S(1)} %shard_map.123.refs_2_), channel_id=1, source_target_pairs={{0,4},{1,5},{2,6},{3,7},{4,0},{5,1},{6,2},{7,3},{8,12},{9,13},{10,... | collective-permute-start | bytes 983048 | tf_op jit(solution)/shard_map/ppermute | solution.py:39
  (64 other events, 386.0 us)
where the time goes:
time: 327 us; the launch traced here: 325 us
  waiting for transfers between devices  157 us (48%)
  starting transfers between devices  118 us (36%)
  Pallas kernels  47.2 us (14%)
    ppermute x42, waiting for transfers between devices, cross(): return lax.ppermute(value, AXES, pairs(steps[stage], steps[1 - stage]))  105 us
    ppermute x24, starting transfers between devices, shift(): return lax.ppermute(value, AXES, pairs(step, step))  67.7 us
    ppermute x21, waiting for transfers between devices, relay(): return lax.ppermute(value, AXES, pairs((0, 0, 0, along), (0, 0, 0, -along)))  40.6 us
    pallas_call x33, Pallas kernels, call(): pl.pallas_call(kernel, in_specs=[smem] * scalars + [vmem] * (len(args) -...  32.9 us
    ppermute x42, starting transfers between devices, cross(): return lax.ppermute(value, AXES, pairs(steps[stage], steps[1 - stage]))  29.4 us
    ppermute x21, starting transfers between devices, relay(): return lax.ppermute(value, AXES, pairs((0, 0, 0, along), (0, 0, 0, -along)))  20.6 us
    ppermute x24, waiting for transfers between devices, shift(): return lax.ppermute(value, AXES, pairs(step, step))  10.8 us
    pallas_call x2, Pallas kernels, inverse_factor(): pl.pallas_call(factor_kernel, in_specs=[vmem], out_specs=vmem, out_shape=...  10.2 us
  transfers between devices with their start and end apart: 87, of which 49 were waited for; matrix products, arithmetic and copies ran while one was open for 0% of the time, Pallas kernels for 8%

commit v1 on v0

--- a/solution.py
+++ b/solution.py
@@ -94,7 +94,7 @@
                 inner = jnp.where(theirs == 0, dx, dy)
                 outer = jnp.where(theirs == 0, dy, dx)
                 piece = jnp.where(outer == 0, 0, jnp.where(outer == 3, 4, 8))
-                swapped = jnp.where(outer == 2, inner * 8 + 5, (piece + inner) * 8 + 4)
+                swapped = jnp.where(outer == 1, inner * 8 + 5, (piece + inner) * 8 + 4)
                 table[r * NPER + s] = jnp.where(theirs == core, inner * 8 + outer, swapped)
 
     lax.fori_loop(0, ROWS, lookup, None)
@@ -239,7 +239,7 @@
         both = wide(o_ref[...])
         edge[pl.ds(TB, TB), :] = fold(dot(both, both, ((0,), (0,))))
     if carries == "pass":
-        head[CARRY, :] = far[2][CARRY, :] + far[5][CARRY, :]
+        head[CARRY, :] = far[1][CARRY, :] + far[5][CARRY, :]
     if carries == "take":
         mine, straight, crossed, opposite = (part[CARRY, :] for part in parts)
         refs[4][...] = (mine + opposite) + (straight + crossed)
@@ -250,7 +250,7 @@
     take_relayed(v_ref, relayed)
     finished_rows(times, index, t_ref, base, v_ref, far, o_ref, wide)
     out[pl.ds(0, TB), :] = fold(dot(wide(block[...]), o_ref[...], ((0,), (0,))))
-    out[pl.ds(TB, TB), :] = far[2][CARRY, :] + far[5][CARRY, :]
+    out[pl.ds(TB, TB), :] = far[1][CARRY, :] + far[5][CARRY, :]
 
 
 CARRY = pl.ds(HEAD * TB, TB)
@@ -320,7 +320,7 @@
 
 def sum_kernel(packed, one, three, two, out):
     rows = pl.ds(0, HEAD * TB)
-    out[rows, :] = three[rows, :]
+    out[rows, :] = one[rows, :]
     out[CARRY, :] = (packed[CARRY, :] + two[CARRY, :]) + (one[CARRY, :] + three[CARRY, :])
 
 
@@ -440,12 +440,12 @@
     forwarded = relay(straight, 1)
     packed = pack(TB, [edge, first[1], first[3], first[2]], carry)
     second = {i: cross(packed, i, 1) for i in (2, 1, 3)}
-    early = pack(HEAD * TB, [packed, second[2], second[1]])
-    late = second[3]
+    early = pack(HEAD * TB, [packed, second[2], second[3]])
+    late = second[1]
     if carry:
         (late,) = call(sum_kernel, [packed, second[1], second[3], second[2]], [tiles_of(HEAD + 1)])
     theirs = [shift(early, dc=1), shift(late, dc=1)]
-    return [straight, crossed, forwarded], [packed, second[1], late, second[2]] + theirs
+    return [straight, crossed, forwarded], [packed, late, second[3], second[2]] + theirs
 
 
 def ring_sum(value, axis):

time: 327 us -> 327 us (level)
  waiting for transfers between devices: 157 us -> 133 us
  starting transfers between devices: 118 us -> 141 us
    ppermute x42, waiting for transfers between devices: 105 us -> 87.1 us  [cross(): return lax.ppermute(value, AXES, pairs(steps[stage], steps[1 - stage]))]
    ppermute x42, starting transfers between devices: 29.4 us -> 44.2 us  [cross(): return lax.ppermute(value, AXES, pairs(steps[stage], steps[1 - stage]))]
    ppermute x24, starting transfers between devices: 67.7 us -> 74.2 us  [shift(): return lax.ppermute(value, AXES, pairs(step, step))]
    ppermute x21, waiting for transfers between devices: 40.6 us -> 35.1 us  [relay(): return lax.ppermute(value, AXES, pairs((0, 0, 0, along), (0, 0, 0, -along)))]
  transfers between devices with their start and end apart: 87 -> 87, of which waited for: 49 -> 55; matrix products, arithmetic and copies ran while one was open for 0% -> 0% of each run, Pallas kernels for 8% -> 9%
where the time goes in v1:
time: 327 us; the launch traced here: 324 us
  starting transfers between devices  141 us (43%)
  waiting for transfers between devices  133 us (41%)
  Pallas kernels  47.2 us (14%)
    ppermute x42, waiting for transfers between devices, cross(): return lax.ppermute(value, AXES, pairs(steps[stage], steps[1 - stage]))  87.1 us
    ppermute x24, starting transfers between devices, shift(): return lax.ppermute(value, AXES, pairs(step, step))  74.2 us
    ppermute x42, starting transfers between devices, cross(): return lax.ppermute(value, AXES, pairs(steps[stage], steps[1 - stage]))  44.2 us
    ppermute x21, waiting for transfers between devices, relay(): return lax.ppermute(value, AXES, pairs((0, 0, 0, along), (0, 0, 0, -along)))  35.1 us
    pallas_call x33, Pallas kernels, call(): pl.pallas_call(kernel, in_specs=[smem] * scalars + [vmem] * (len(args) -...  32.9 us
    ppermute x21, starting transfers between devices, relay(): return lax.ppermute(value, AXES, pairs((0, 0, 0, along), (0, 0, 0, -along)))  22.3 us
    ppermute x24, waiting for transfers between devices, shift(): return lax.ppermute(value, AXES, pairs(step, step))  11.1 us
    pallas_call x2, Pallas kernels, inverse_factor(): pl.pallas_call(factor_kernel, in_specs=[vmem], out_specs=vmem, out_shape=...  10.2 us
  transfers between devices with their start and end apart: 87, of which 55 were waited for; matrix products, arithmetic and copies ran while one was open for 0% of the time, Pallas kernels for 9%

profile of v1, /device:TPU:1, one launch (start us, length us, event | category | flops | bytes accessed | tf_op | source)
XLA Modules:
  0.0 324.2 jit_solution(4494792059581884947)
XLA Ops:
  28.7 4.3 %collective-permute-done.straight = f32[512,128]{1,0:T(8,128)} collective-permute-done((f32[512,128]{1,0:T(8,128)S(1)}, f32[512,128]{1,0:T(8,128)}, u32[]{:S(2)}, u32[]{:S(2)}) %collective-permute-start) | collective-permute-done | bytes 262176 | tf_op jit(solution)/shard_map/ppermute | solution.py:433
  36.5 4.0 %prepare.1 = (bf16[8,256,128]{2,1,0:T(8,128)(2,1)S(1)}, bf16[8,3,256,256]{3,2,1,0:T(8,128)(2,1)S(1)}, s32[49]{0:T(128)S(1)}) custom-call(s32[48]{0:T(128)} %near_src.1, s32[48]{0:T(128)} %near_mask.1, s32[8]{0:T(128)} %far_src.1, s32[8]{0:T(128)} %far_mask.1, s32[2]{0:T(128)S(1)} %pad_add_fusion.here, f32[48,128,128]{2,1,0:T(8,128)} %near.1, f32[8,128,128]{2,1,0:T(8,128)} %far.1), custom_call_target="tpu_custom_call" | custom-call | tf_op jit(solution)/shard_map/prepare/pallas_call | solution.py:122
  56.0 5.2 %collective-permute-done.18.refs_1_.refs_3_ = f32[512,128]{1,0:T(8,128)S(1)} collective-permute-done((f32[512,128]{1,0:T(8,128)S(1)}, f32[512,128]{1,0:T(8,128)S(1)}, u32[]{:S(2)}, u32[]{:S(2)}) %collective-permute-start.18) | collective-permute-done | bytes 262176 | tf_op jit(solution)/shard_map/ppermute | solution.py:44
  61.5 4.3 %collective-permute-start.19 = (f32[1536,128]{1,0:T(8,128)S(1)}, f32[1536,128]{1,0:T(8,128)S(1)}, u32[]{:S(2)}, u32[]{:S(2)}) collective-permute-start(f32[1536,128]{1,0:T(8,128)S(1)} %shard_map.101), channel_id=1, source_target_pairs={{0,4},{1,5},{2,6},{3,7},{4,0},{5,1},{6,2},{7,3},{8,12},{9,13},{10,... | collective-permute-start | bytes 2359304 | tf_op jit(solution)/shard_map/ppermute | solution.py:39
  67.2 4.8 %collective-permute-done.11.straight = f32[512,128]{1,0:T(8,128)S(1)} collective-permute-done((f32[512,128]{1,0:T(8,128)S(1)}, f32[512,128]{1,0:T(8,128)S(1)}, u32[]{:S(2)}, u32[]{:S(2)}) %collective-permute-start.11) | collective-permute-done | bytes 262176 | tf_op jit(solution)/shard_map/ppermute | solution.py:433
  88.8 6.5 %collective-permute-done.29.refs_1_.refs_3_ = f32[512,128]{1,0:T(8,128)S(1)} collective-permute-done((f32[512,128]{1,0:T(8,128)S(1)}, f32[512,128]{1,0:T(8,128)S(1)}, u32[]{:S(2)}, u32[]{:S(2)}) %collective-permute-start.29) | collective-permute-done | bytes 262176 | tf_op jit(solution)/shard_map/ppermute | solution.py:44
  95.6 9.7 %collective-permute-start.30 = (f32[1536,128]{1,0:T(8,128)S(1)}, f32[1536,128]{1,0:T(8,128)S(1)}, u32[]{:S(2)}, u32[]{:S(2)}) collective-permute-start(f32[1536,128]{1,0:T(8,128)S(1)} %shard_map.105), channel_id=1, source_target_pairs={{0,4},{1,5},{2,6},{3,7},{4,0},{5,1},{6,2},{7,3},{8,12},{9,13},{10,... | collective-permute-start | bytes 2359304 | tf_op jit(solution)/shard_map/ppermute | solution.py:39
  106.8 5.0 %collective-permute-done.22.straight = f32[512,128]{1,0:T(8,128)S(1)} collective-permute-done((f32[512,128]{1,0:T(8,128)S(1)}, f32[512,128]{1,0:T(8,128)S(1)}, u32[]{:S(2)}, u32[]{:S(2)}) %collective-permute-start.22) | collective-permute-done | bytes 262176 | tf_op jit(solution)/shard_map/ppermute | solution.py:433
  130.6 6.3 %collective-permute-done.40.two.refs_1_.refs_3_ = f32[640,128]{1,0:T(8,128)S(1)} collective-permute-done((f32[640,128]{1,0:T(8,128)S(1)}, f32[640,128]{1,0:T(8,128)S(1)}, u32[]{:S(2)}, u32[]{:S(2)}) %collective-permute-start.40) | collective-permute-done | bytes 327712 | tf_op jit(solution)/shard_map/ppermute | solution.py:44
  138.1 9.7 %collective-permute-start.41 = (f32[1536,128]{1,0:T(8,128)S(1)}, f32[1536,128]{1,0:T(8,128)S(1)}, u32[]{:S(2)}, u32[]{:S(2)}) collective-permute-start(f32[1536,128]{1,0:T(8,128)S(1)} %shard_map.110), channel_id=1, source_target_pairs={{0,4},{1,5},{2,6},{3,7},{4,0},{5,1},{6,2},{7,3},{8,12},{9,13},{10,... | collective-permute-start | bytes 2359304 | tf_op jit(solution)/shard_map/ppermute | solution.py:39
  150.1 5.4 %collective-permute-done.38.one = f32[640,128]{1,0:T(8,128)S(1)} collective-permute-done((f32[640,128]{1,0:T(8,128)S(1)}, f32[640,128]{1,0:T(8,128)S(1)}, u32[]{:S(2)}, u32[]{:S(2)}) %collective-permute-start.38) | collective-permute-done | bytes 327712 | tf_op jit(solution)/shard_map/ppermute | solution.py:44
  159.0 6.0 %collective-permute-done.34.crossed = f32[512,128]{1,0:T(8,128)S(1)} collective-permute-done((f32[512,128]{1,0:T(8,128)S(1)}, f32[512,128]{1,0:T(8,128)S(1)}, u32[]{:S(2)}, u32[]{:S(2)}) %collective-permute-start.34) | collective-permute-done | bytes 262176 | tf_op jit(solution)/shard_map/ppermute | solution.py:433
  185.2 4.1 %collective-permute-start.52 = (f32[1536,128]{1,0:T(8,128)S(1)}, f32[1536,128]{1,0:T(8,128)S(1)}, u32[]{:S(2)}, u32[]{:S(2)}) collective-permute-start(f32[1536,128]{1,0:T(8,128)S(1)} %shard_map.114), channel_id=1, source_target_pairs={{0,4},{1,5},{2,6},{3,7},{4,0},{5,1},{6,2},{7,3},{8,12},{9,13},{10,... | collective-permute-start | bytes 2359304 | tf_op jit(solution)/shard_map/ppermute | solution.py:39
  190.8 4.8 %collective-permute-done.44.straight.refs_9_ = f32[640,128]{1,0:T(8,128)S(1)} collective-permute-done((f32[640,128]{1,0:T(8,128)S(1)}, f32[640,128]{1,0:T(8,128)S(1)}, u32[]{:S(2)}, u32[]{:S(2)}) %collective-permute-start.44) | collective-permute-done | bytes 327712 | tf_op jit(solution)/shard_map/ppermute | solution.py:433
  196.7 4.5 %collective-permute-start.53 = (f32[512,128]{1,0:T(8,128)S(1)}, f32[512,128]{1,0:T(8,128)S(1)}, u32[]{:S(2)}, u32[]{:S(2)}) collective-permute-start(f32[512,128]{1,0:T(8,128)S(1)} %collective-permute-done.49.refs_1_), channel_id=1, source_target_pairs={{0,4},{1,5},{2,6},{3,7},{4,0},{5,1},{6,2},{7,3},{8,12},{9,13},{10,... | collective-permute-start | bytes 786440 | tf_op jit(solution)/shard_map/ppermute | solution.py:39
  214.7 6.5 %collective-permute-done.62.refs_1_.refs_3_ = f32[512,128]{1,0:T(8,128)S(1)} collective-permute-done((f32[512,128]{1,0:T(8,128)S(1)}, f32[512,128]{1,0:T(8,128)S(1)}, u32[]{:S(2)}, u32[]{:S(2)}) %collective-permute-start.62) | collective-permute-done | bytes 262176 | tf_op jit(solution)/shard_map/ppermute | solution.py:44
  221.2 9.7 %collective-permute-start.63 = (f32[1536,128]{1,0:T(8,128)S(1)}, f32[1536,128]{1,0:T(8,128)S(1)}, u32[]{:S(2)}, u32[]{:S(2)}) collective-permute-start(f32[1536,128]{1,0:T(8,128)S(1)} %shard_map.118), channel_id=1, source_target_pairs={{0,4},{1,5},{2,6},{3,7},{4,0},{5,1},{6,2},{7,3},{8,12},{9,13},{10,... | collective-permute-start | bytes 2359304 | tf_op jit(solution)/shard_map/ppermute | solution.py:39
  232.3 5.0 %collective-permute-done.55.straight = f32[512,128]{1,0:T(8,128)S(1)} collective-permute-done((f32[512,128]{1,0:T(8,128)S(1)}, f32[512,128]{1,0:T(8,128)S(1)}, u32[]{:S(2)}, u32[]{:S(2)}) %collective-permute-start.55) | collective-permute-done | bytes 262176 | tf_op jit(solution)/shard_map/ppermute | solution.py:433
  240.8 5.1 %factor.2.inverse.first = f32[128,128]{1,0:T(8,128)S(1)} custom-call(f32[128,128]{1,0:T(8,128)S(1)} %get-tuple-element.79.gram), custom_call_target="tpu_custom_call" | custom-call | tf_op jit(solution)/shard_map/factor/pallas_call | solution.py:404
  261.9 5.7 %collective-permute-done.73.two.refs_1_.refs_3_ = f32[640,128]{1,0:T(8,128)S(1)} collective-permute-done((f32[640,128]{1,0:T(8,128)S(1)}, f32[640,128]{1,0:T(8,128)S(1)}, u32[]{:S(2)}, u32[]{:S(2)}) %collective-permute-start.73) | collective-permute-done | bytes 327712 | tf_op jit(solution)/shard_map/ppermute | solution.py:44
  268.3 4.9 %collective-permute-start.74 = (f32[1536,128]{1,0:T(8,128)S(1)}, f32[1536,128]{1,0:T(8,128)S(1)}, u32[]{:S(2)}, u32[]{:S(2)}) collective-permute-start(f32[1536,128]{1,0:T(8,128)S(1)} %shard_map.124), channel_id=1, source_target_pairs={{0,4},{1,5},{2,6},{3,7},{4,0},{5,1},{6,2},{7,3},{8,12},{9,13},{10,... | collective-permute-start | bytes 2359304 | tf_op jit(solution)/shard_map/ppermute | solution.py:39
  275.3 5.3 %collective-permute-done.71.one = f32[640,128]{1,0:T(8,128)S(1)} collective-permute-done((f32[640,128]{1,0:T(8,128)S(1)}, f32[640,128]{1,0:T(8,128)S(1)}, u32[]{:S(2)}, u32[]{:S(2)}) %collective-permute-start.71) | collective-permute-done | bytes 327712 | tf_op jit(solution)/shard_map/ppermute | solution.py:44
  298.4 4.9 %collective-permute-done.78 = f32[256,128]{1,0:T(8,128)S(1)} collective-permute-done((f32[256,128]{1,0:T(8,128)S(1)}, f32[256,128]{1,0:T(8,128)S(1)}, u32[]{:S(2)}, u32[]{:S(2)}) %collective-permute-start.78) | collective-permute-done | bytes 131104 | tf_op jit(solution)/shard_map/ppermute | solution.py:39
  316.5 5.1 %factor.3.inverse.second = f32[128,128]{1,0:T(8,128)S(1)} custom-call(f32[128,128]{1,0:T(8,128)S(1)} %get-tuple-element.87.gram), custom_call_target="tpu_custom_call" | custom-call | tf_op jit(solution)/shard_map/factor/pallas_call | solution.py:404
  (195 shorter events, 185.6 us)
Async XLA Ops:
  21.2 22.0 %collective-permute-start.8 = (f32[1536,128]{1,0:T(8,128)S(1)}, f32[1536,128]{1,0:T(8,128)S(1)}, u32[]{:S(2)}, u32[]{:S(2)}) collective-permute-start(f32[1536,128]{1,0:T(8,128)S(1)} %shard_map.97), channel_id=1, source_target_pairs={{0,4},{1,5},{2,6},{3,7},{4,0},{5,1},{6,2},{7,3},{8,12},{9,13},{10,... | collective-permute-start | bytes 2359304 | tf_op jit(solution)/shard_map/ppermute | solution.py:39
  28.6 11.9 %collective-permute-start.1 = (f32[512,128]{1,0:T(8,128)S(1)}, f32[512,128]{1,0:T(8,128)}, u32[]{:S(2)}, u32[]{:S(2)}) collective-permute-start(f32[512,128]{1,0:T(8,128)S(1)} %get-tuple-element.47.head.refs_0_), channel_id=1, source_target_pairs={{0,3},{1,0},{2,1},{3,2},{4,5},{5,6},{6,7},{7,4},{8,11},{9,8},{10,9... | collective-permute-start | bytes 786440 | tf_op jit(solution)/shard_map/ppermute | solution.py:433
  33.0 10.2 %collective-permute-start.10 = (f32[512,128]{1,0:T(8,128)}, f32[512,128]{1,0:T(8,128)S(1)}, u32[]{:S(2)}, u32[]{:S(2)}) collective-permute-start(f32[512,128]{1,0:T(8,128)} %collective-permute-done.straight), channel_id=1, source_target_pairs={{0,1},{1,2},{2,3},{3,0},{4,7},{5,4},{6,5},{7,6},{8,9},{9,10},{10,1... | collective-permute-start | bytes 786440 | tf_op jit(solution)/shard_map/ppermute | solution.py:433
  61.5 16.2 %collective-permute-start.19 = (f32[1536,128]{1,0:T(8,128)S(1)}, f32[1536,128]{1,0:T(8,128)S(1)}, u32[]{:S(2)}, u32[]{:S(2)}) collective-permute-start(f32[1536,128]{1,0:T(8,128)S(1)} %shard_map.101), channel_id=1, source_target_pairs={{0,4},{1,5},{2,6},{3,7},{4,0},{5,1},{6,2},{7,3},{8,12},{9,13},{10,... | collective-permute-start | bytes 2359304 | tf_op jit(solution)/shard_map/ppermute | solution.py:39
  66.1 9.9 %collective-permute-start.12 = (f32[512,128]{1,0:T(8,128)S(1)}, f32[512,128]{1,0:T(8,128)S(1)}, u32[]{:S(2)}, u32[]{:S(2)}) collective-permute-start(f32[512,128]{1,0:T(8,128)S(1)} %get-tuple-element.52.head.refs_0_), channel_id=1, source_target_pairs={{0,3},{1,0},{2,1},{3,2},{4,5},{5,6},{6,7},{7,4},{8,11},{9,8},{10,9... | collective-permute-start | bytes 786440 | tf_op jit(solution)/shard_map/ppermute | solution.py:433
  95.6 21.4 %collective-permute-start.30 = (f32[1536,128]{1,0:T(8,128)S(1)}, f32[1536,128]{1,0:T(8,128)S(1)}, u32[]{:S(2)}, u32[]{:S(2)}) collective-permute-start(f32[1536,128]{1,0:T(8,128)S(1)} %shard_map.105), channel_id=1, source_target_pairs={{0,4},{1,5},{2,6},{3,7},{4,0},{5,1},{6,2},{7,3},{8,12},{9,13},{10,... | collective-permute-start | bytes 2359304 | tf_op jit(solution)/shard_map/ppermute | solution.py:39
  105.3 9.9 %collective-permute-start.23 = (f32[512,128]{1,0:T(8,128)S(1)}, f32[512,128]{1,0:T(8,128)S(1)}, u32[]{:S(2)}, u32[]{:S(2)}) collective-permute-start(f32[512,128]{1,0:T(8,128)S(1)} %get-tuple-element.57.head), channel_id=1, source_target_pairs={{0,3},{1,0},{2,1},{3,2},{4,5},{5,6},{6,7},{7,4},{8,11},{9,8},{10,9... | collective-permute-start | bytes 786440 | tf_op jit(solution)/shard_map/ppermute | solution.py:433
  128.8 9.3 %collective-permute-start.39 = (f32[640,128]{1,0:T(8,128)S(1)}, f32[640,128]{1,0:T(8,128)S(1)}, u32[]{:S(2)}, u32[]{:S(2)}) collective-permute-start(f32[640,128]{1,0:T(8,128)S(1)} %shard_map.108.packed.refs_0_), channel_id=1, source_target_pairs={{0,96},{1,97},{2,98},{3,99},{4,28},{5,29},{6,30},{7,31},{8,104},{9... | collective-permute-start | bytes 983048 | tf_op jit(solution)/shard_map/ppermute | solution.py:44
  138.1 28.4 %collective-permute-start.41 = (f32[1536,128]{1,0:T(8,128)S(1)}, f32[1536,128]{1,0:T(8,128)S(1)}, u32[]{:S(2)}, u32[]{:S(2)}) collective-permute-start(f32[1536,128]{1,0:T(8,128)S(1)} %shard_map.110), channel_id=1, source_target_pairs={{0,4},{1,5},{2,6},{3,7},{4,0},{5,1},{6,2},{7,3},{8,12},{9,13},{10,... | collective-permute-start | bytes 2359304 | tf_op jit(solution)/shard_map/ppermute | solution.py:39
  155.5 11.0 %collective-permute-start.42 = (f32[640,128]{1,0:T(8,128)S(1)}, f32[640,128]{1,0:T(8,128)S(1)}, u32[]{:S(2)}, u32[]{:S(2)}) collective-permute-start(f32[640,128]{1,0:T(8,128)S(1)} %shard_map.109.refs_1_), channel_id=1, source_target_pairs={{0,4},{1,5},{2,6},{3,7},{4,0},{5,1},{6,2},{7,3},{8,12},{9,13},{10,... | collective-permute-start | bytes 983048 | tf_op jit(solution)/shard_map/ppermute | solution.py:39
  156.3 8.7 %collective-permute-start.34 = (f32[512,128]{1,0:T(8,128)S(1)}, f32[512,128]{1,0:T(8,128)S(1)}, u32[]{:S(2)}, u32[]{:S(2)}) collective-permute-start(f32[512,128]{1,0:T(8,128)S(1)} %get-tuple-element.62.head.refs_0_), channel_id=1, source_target_pairs={{0,3},{1,0},{2,1},{3,2},{4,5},{5,6},{6,7},{7,4},{8,11},{9,8},{10,9... | collective-permute-start | bytes 786440 | tf_op jit(solution)/shard_map/ppermute | solution.py:433
  157.0 9.6 %collective-permute-start.43 = (f32[512,128]{1,0:T(8,128)S(1)}, f32[512,128]{1,0:T(8,128)S(1)}, u32[]{:S(2)}, u32[]{:S(2)}) collective-permute-start(f32[512,128]{1,0:T(8,128)S(1)} %collective-permute-done.33.straight), channel_id=1, source_target_pairs={{0,1},{1,2},{2,3},{3,0},{4,7},{5,4},{6,5},{7,6},{8,9},{9,10},{10,1... | collective-permute-start | bytes 786440 | tf_op jit(solution)/shard_map/ppermute | solution.py:433
  176.6 8.5 %collective-permute-start.50 = (f32[512,128]{1,0:T(8,128)S(1)}, f32[512,128]{1,0:T(8,128)S(1)}, u32[]{:S(2)}, u32[]{:S(2)}) collective-permute-start(f32[512,128]{1,0:T(8,128)S(1)} %shard_map.113.refs_0_), channel_id=1, source_target_pairs={{0,96},{1,97},{2,98},{3,99},{4,28},{5,29},{6,30},{7,31},{8,104},{9... | collective-permute-start | bytes 786440 | tf_op jit(solution)/shard_map/ppermute | solution.py:44
  185.2 18.0 %collective-permute-start.52 = (f32[1536,128]{1,0:T(8,128)S(1)}, f32[1536,128]{1,0:T(8,128)S(1)}, u32[]{:S(2)}, u32[]{:S(2)}) collective-permute-start(f32[1536,128]{1,0:T(8,128)S(1)} %shard_map.114), channel_id=1, source_target_pairs={{0,4},{1,5},{2,6},{3,7},{4,0},{5,1},{6,2},{7,3},{8,12},{9,13},{10,... | collective-permute-start | bytes 2359304 | tf_op jit(solution)/shard_map/ppermute | solution.py:39
  189.3 11.9 %collective-permute-start.45 = (f32[640,128]{1,0:T(8,128)S(1)}, f32[640,128]{1,0:T(8,128)S(1)}, u32[]{:S(2)}, u32[]{:S(2)}) collective-permute-start(f32[640,128]{1,0:T(8,128)S(1)} %get-tuple-element.67.head.refs_8_.refs_0_), channel_id=1, source_target_pairs={{0,3},{1,0},{2,1},{3,2},{4,5},{5,6},{6,7},{7,4},{8,11},{9,8},{10,9... | collective-permute-start | bytes 983048 | tf_op jit(solution)/shard_map/ppermute | solution.py:433
  221.2 26.3 %collective-permute-start.63 = (f32[1536,128]{1,0:T(8,128)S(1)}, f32[1536,128]{1,0:T(8,128)S(1)}, u32[]{:S(2)}, u32[]{:S(2)}) collective-permute-start(f32[1536,128]{1,0:T(8,128)S(1)} %shard_map.118), channel_id=1, source_target_pairs={{0,4},{1,5},{2,6},{3,7},{4,0},{5,1},{6,2},{7,3},{8,12},{9,13},{10,... | collective-permute-start | bytes 2359304 | tf_op jit(solution)/shard_map/ppermute | solution.py:39
  230.9 15.1 %collective-permute-start.56 = (f32[512,128]{1,0:T(8,128)S(1)}, f32[512,128]{1,0:T(8,128)S(1)}, u32[]{:S(2)}, u32[]{:S(2)}) collective-permute-start(f32[512,128]{1,0:T(8,128)S(1)} %get-tuple-element.72.head), channel_id=1, source_target_pairs={{0,3},{1,0},{2,1},{3,2},{4,5},{5,6},{6,7},{7,4},{8,11},{9,8},{10,9... | collective-permute-start | bytes 786440 | tf_op jit(solution)/shard_map/ppermute | solution.py:433
  237.4 10.1 %collective-permute-start.65 = (f32[512,128]{1,0:T(8,128)S(1)}, f32[512,128]{1,0:T(8,128)S(1)}, u32[]{:S(2)}, u32[]{:S(2)}) collective-permute-start(f32[512,128]{1,0:T(8,128)S(1)} %collective-permute-done.55.straight), channel_id=1, source_target_pairs={{0,1},{1,2},{2,3},{3,0},{4,7},{5,4},{6,5},{7,6},{8,9},{9,10},{10,1... | collective-permute-start | bytes 786440 | tf_op jit(solution)/shard_map/ppermute | solution.py:433
  237.6 9.9 %collective-permute-start.64 = (f32[512,128]{1,0:T(8,128)S(1)}, f32[512,128]{1,0:T(8,128)S(1)}, u32[]{:S(2)}, u32[]{:S(2)}) collective-permute-start(f32[512,128]{1,0:T(8,128)S(1)} %collective-permute-done.60.refs_1_), channel_id=1, source_target_pairs={{0,4},{1,5},{2,6},{3,7},{4,0},{5,1},{6,2},{7,3},{8,12},{9,13},{10,... | collective-permute-start | bytes 786440 | tf_op jit(solution)/shard_map/ppermute | solution.py:39
  268.3 22.2 %collective-permute-start.74 = (f32[1536,128]{1,0:T(8,128)S(1)}, f32[1536,128]{1,0:T(8,128)S(1)}, u32[]{:S(2)}, u32[]{:S(2)}) collective-permute-start(f32[1536,128]{1,0:T(8,128)S(1)} %shard_map.124), channel_id=1, source_target_pairs={{0,4},{1,5},{2,6},{3,7},{4,0},{5,1},{6,2},{7,3},{8,12},{9,13},{10,... | collective-permute-start | bytes 2359304 | tf_op jit(solution)/shard_map/ppermute | solution.py:39
  273.2 8.5 %collective-permute-start.66 = (f32[512,128]{1,0:T(8,128)S(1)}, f32[512,128]{1,0:T(8,128)S(1)}, u32[]{:S(2)}, u32[]{:S(2)}) collective-permute-start(f32[512,128]{1,0:T(8,128)S(1)} %get-tuple-element.77.head), channel_id=1, source_target_pairs={{0,1},{1,2},{2,3},{3,0},{4,7},{5,4},{6,5},{7,6},{8,9},{9,10},{10,1... | collective-permute-start | bytes 786440 | tf_op jit(solution)/shard_map/ppermute | solution.py:433
  280.7 9.8 %collective-permute-start.75 = (f32[640,128]{1,0:T(8,128)S(1)}, f32[640,128]{1,0:T(8,128)S(1)}, u32[]{:S(2)}, u32[]{:S(2)}) collective-permute-start(f32[640,128]{1,0:T(8,128)S(1)} %shard_map.123.refs_1_), channel_id=1, source_target_pairs={{0,4},{1,5},{2,6},{3,7},{4,0},{5,1},{6,2},{7,3},{8,12},{9,13},{10,... | collective-permute-start | bytes 983048 | tf_op jit(solution)/shard_map/ppermute | solution.py:39
  281.7 8.8 %collective-permute-start.76 = (f32[512,128]{1,0:T(8,128)S(1)}, f32[512,128]{1,0:T(8,128)S(1)}, u32[]{:S(2)}, u32[]{:S(2)}) collective-permute-start(f32[512,128]{1,0:T(8,128)S(1)} %collective-permute-done.66.straight), channel_id=1, source_target_pairs={{0,1},{1,2},{2,3},{3,0},{4,7},{5,4},{6,5},{7,6},{8,9},{9,10},{10,1... | collective-permute-start | bytes 786440 | tf_op jit(solution)/shard_map/ppermute | solution.py:433
  313.6 9.4 %collective-permute-start.86 = (f32[128,128]{1,0:T(8,128)S(1)}, f32[128,128]{1,0:T(8,128)S(1)}, u32[]{:S(2)}, u32[]{:S(2)}) collective-permute-start(f32[128,128]{1,0:T(8,128)S(1)} %add_add_fusion.2), channel_id=1, source_target_pairs={{0,96},{1,97},{2,98},{3,99},{4,100},{5,101},{6,102},{7,103},{8,104... | collective-permute-start | bytes 196616 | tf_op jit(solution)/shard_map/ppermute | solution.py:39
  (64 other events, 379.9 us)

commit v2 on v1

--- a/solution.py
+++ b/solution.py
@@ -110,7 +110,7 @@
                 tile = near_v[slot] * near_mask[slot].astype(jnp.float32)
             else:
                 tile = far_v[r] * far_mask[r].astype(jnp.float32)
-            t_ref[r, s // 2, :, pl.ds((s % 2) * TB, TB)] = tall(tile)
+            t_ref[r, :, pl.ds(s * TB, TB)] = tall(tile)
 
     lax.fori_loop(0, ROWS, convert, None)
 
@@ -125,7 +125,7 @@
         out_specs=[vmem, vmem, smem],
         out_shape=[
             jax.ShapeDtypeStruct((ROWS, 2 * TB, TB), jnp.bfloat16),
-            jax.ShapeDtypeStruct((ROWS, NPER // 2, 2 * TB, 2 * TB), jnp.bfloat16),
+            jax.ShapeDtypeStruct((ROWS, 2 * TB, NPER * TB), jnp.bfloat16),
             jax.ShapeDtypeStruct((ROWS * NPER + 1,), jnp.int32),
         ],
         scratch_shapes=[
@@ -213,11 +213,7 @@
     def half(h, _):
         for t in range(STEP):
             r = h * STEP + t
-            acc = None
-            for p in range(NPER // 2):
-                rhs = jnp.concatenate([source(r, 2 * p), source(r, 2 * p + 1)], axis=0)
-                part = dot(t_ref[r, p], rhs, ((1,), (0,)))
-                acc = part if acc is None else acc + part
+            acc = dot(t_ref[r], jnp.concatenate([source(r, s) for s in range(NPER)], axis=0), ((1,), (0,)))
             out[tile_rows(r), :] = store(base[tile_rows(r), :] + times * fold(acc))
 
     lax.fori_loop(0, ROWS // STEP, half, None)
@@ -412,8 +408,9 @@
     )(gram)
 
 
-def encode_kernel(block, inverse, out):
+def encode_kernel(block, first, inverse, out, both):
     inv = tall(inverse[...])
+    both[...] = fold(dot(inv, wide(first[...]), ((1,), (0,))))
 
     def step(h, _):
         for t in range(HEAD):
@@ -423,10 +420,9 @@
     lax.fori_loop(0, ROWS // HEAD, step, None)
 
 
-def rayleigh_kernel(projection, first, second, out):
-    inv = tall(second[...])
-    right = times_transpose(projection[...] * (1.0 / NODES), tall(first[...]))
-    out[...] = times_transpose(fold(dot(inv, wide(right), ((1,), (0,)))), inv)
+def rayleigh_kernel(projection, second, both, out):
+    left = fold(dot(tall(second[...]), wide(projection[...] * (1.0 / NODES)), ((1,), (0,))))
+    out[...] = times_transpose(left, tall(both[...]))
 
 
 def relay(value, along):
@@ -485,11 +481,11 @@
                 (gram,) = total
     value = ring_sum(value, "z")
     second = inverse_factor(value[TB:])
-    (encodings,) = call(encode_kernel, [block, second], [BLOCK])
+    encodings, both = call(encode_kernel, [block, inverse, second], [BLOCK, SMALL])
     projection = value[:TB]
     projection = projection + shift(projection, dc=1)
     projection = ring_sum(ring_sum(projection, "x"), "y")
-    (rayleigh,) = call(rayleigh_kernel, [projection, inverse, second], [SMALL])
+    (rayleigh,) = call(rayleigh_kernel, [projection, second, both], [SMALL])
     return encodings, rayleigh
 
 

time: 327 us -> 326 us (level)
  no operation moved by 1% of the time
where the time goes in v2:
time: 326 us; the launch traced here: 324 us
  starting transfers between devices  140 us (43%)
  waiting for transfers between devices  133 us (41%)
  Pallas kernels  47.3 us (15%)
    ppermute x42, waiting for transfers between devices, cross(): return lax.ppermute(value, AXES, pairs(steps[stage], steps[1 - stage]))  87 us
    ppermute x24, starting transfers between devices, shift(): return lax.ppermute(value, AXES, pairs(step, step))  74.3 us
    ppermute x42, starting transfers between devices, cross(): return lax.ppermute(value, AXES, pairs(steps[stage], steps[1 - stage]))  43.9 us
    ppermute x21, waiting for transfers between devices, relay(): return lax.ppermute(value, AXES, pairs((0, 0, 0, along), (0, 0, 0, -along)))  35.4 us
    pallas_call x33, Pallas kernels, call(): pl.pallas_call(kernel, in_specs=[smem] * scalars + [vmem] * (len(args) -...  33 us
    ppermute x21, starting transfers between devices, relay(): return lax.ppermute(value, AXES, pairs((0, 0, 0, along), (0, 0, 0, -along)))  22.2 us
    ppermute x24, waiting for transfers between devices, shift(): return lax.ppermute(value, AXES, pairs(step, step))  11.1 us
    pallas_call x2, Pallas kernels, inverse_factor(): pl.pallas_call(factor_kernel, in_specs=[vmem], out_specs=vmem, out_shape=...  10.2 us
  transfers between devices with their start and end apart: 87, of which 55 were waited for; matrix products, arithmetic and copies ran while one was open for 0% of the time, Pallas kernels for 9%

profile of v2, /device:TPU:1, one launch (start us, length us, event | category | flops | bytes accessed | tf_op | source)
XLA Modules:
  0.0 324.2 jit_solution(451590330340895213)
XLA Ops:
  28.7 4.3 %collective-permute-done.straight = f32[512,128]{1,0:T(8,128)} collective-permute-done((f32[512,128]{1,0:T(8,128)S(1)}, f32[512,128]{1,0:T(8,128)}, u32[]{:S(2)}, u32[]{:S(2)}) %collective-permute-start) | collective-permute-done | bytes 262176 | tf_op jit(solution)/shard_map/ppermute | solution.py:429
  36.5 4.0 %prepare.1 = (bf16[8,256,128]{2,1,0:T(8,128)(2,1)S(1)}, bf16[8,256,768]{2,1,0:T(8,128)(2,1)S(1)}, s32[49]{0:T(128)S(1)}) custom-call(s32[48]{0:T(128)} %near_src.1, s32[48]{0:T(128)} %near_mask.1, s32[8]{0:T(128)} %far_src.1, s32[8]{0:T(128)} %far_mask.1, s32[2]{0:T(128)S(1)} %pad_add_fusion.here, f32[48,128,128]{2,1,0:T(8,128)} %near.1, f32[8,128,128]{2,1,0:T(8,128)} %far.1), custom_call_target="tpu_custom_call" | custom-call | tf_op jit(solution)/shard_map/prepare/pallas_call | solution.py:122
  56.0 5.2 %collective-permute-done.18.refs_1_.refs_3_ = f32[512,128]{1,0:T(8,128)S(1)} collective-permute-done((f32[512,128]{1,0:T(8,128)S(1)}, f32[512,128]{1,0:T(8,128)S(1)}, u32[]{:S(2)}, u32[]{:S(2)}) %collective-permute-start.18) | collective-permute-done | bytes 262176 | tf_op jit(solution)/shard_map/ppermute | solution.py:44
  61.5 4.3 %collective-permute-start.19 = (f32[1536,128]{1,0:T(8,128)S(1)}, f32[1536,128]{1,0:T(8,128)S(1)}, u32[]{:S(2)}, u32[]{:S(2)}) collective-permute-start(f32[1536,128]{1,0:T(8,128)S(1)} %shard_map.101), channel_id=1, source_target_pairs={{0,4},{1,5},{2,6},{3,7},{4,0},{5,1},{6,2},{7,3},{8,12},{9,13},{10,... | collective-permute-start | bytes 2359304 | tf_op jit(solution)/shard_map/ppermute | solution.py:39
  67.2 4.8 %collective-permute-done.11.straight = f32[512,128]{1,0:T(8,128)S(1)} collective-permute-done((f32[512,128]{1,0:T(8,128)S(1)}, f32[512,128]{1,0:T(8,128)S(1)}, u32[]{:S(2)}, u32[]{:S(2)}) %collective-permute-start.11) | collective-permute-done | bytes 262176 | tf_op jit(solution)/shard_map/ppermute | solution.py:429
  88.8 6.5 %collective-permute-done.29.refs_1_.refs_3_ = f32[512,128]{1,0:T(8,128)S(1)} collective-permute-done((f32[512,128]{1,0:T(8,128)S(1)}, f32[512,128]{1,0:T(8,128)S(1)}, u32[]{:S(2)}, u32[]{:S(2)}) %collective-permute-start.29) | collective-permute-done | bytes 262176 | tf_op jit(solution)/shard_map/ppermute | solution.py:44
  95.6 9.7 %collective-permute-start.30 = (f32[1536,128]{1,0:T(8,128)S(1)}, f32[1536,128]{1,0:T(8,128)S(1)}, u32[]{:S(2)}, u32[]{:S(2)}) collective-permute-start(f32[1536,128]{1,0:T(8,128)S(1)} %shard_map.105), channel_id=1, source_target_pairs={{0,4},{1,5},{2,6},{3,7},{4,0},{5,1},{6,2},{7,3},{8,12},{9,13},{10,... | collective-permute-start | bytes 2359304 | tf_op jit(solution)/shard_map/ppermute | solution.py:39
  106.8 5.0 %collective-permute-done.22.straight = f32[512,128]{1,0:T(8,128)S(1)} collective-permute-done((f32[512,128]{1,0:T(8,128)S(1)}, f32[512,128]{1,0:T(8,128)S(1)}, u32[]{:S(2)}, u32[]{:S(2)}) %collective-permute-start.22) | collective-permute-done | bytes 262176 | tf_op jit(solution)/shard_map/ppermute | solution.py:429
  130.6 6.3 %collective-permute-done.40.two.refs_1_.refs_3_ = f32[640,128]{1,0:T(8,128)S(1)} collective-permute-done((f32[640,128]{1,0:T(8,128)S(1)}, f32[640,128]{1,0:T(8,128)S(1)}, u32[]{:S(2)}, u32[]{:S(2)}) %collective-permute-start.40) | collective-permute-done | bytes 327712 | tf_op jit(solution)/shard_map/ppermute | solution.py:44
  138.2 9.7 %collective-permute-start.41 = (f32[1536,128]{1,0:T(8,128)S(1)}, f32[1536,128]{1,0:T(8,128)S(1)}, u32[]{:S(2)}, u32[]{:S(2)}) collective-permute-start(f32[1536,128]{1,0:T(8,128)S(1)} %shard_map.110), channel_id=1, source_target_pairs={{0,4},{1,5},{2,6},{3,7},{4,0},{5,1},{6,2},{7,3},{8,12},{9,13},{10,... | collective-permute-start | bytes 2359304 | tf_op jit(solution)/shard_map/ppermute | solution.py:39
  150.1 5.4 %collective-permute-done.38.one = f32[640,128]{1,0:T(8,128)S(1)} collective-permute-done((f32[640,128]{1,0:T(8,128)S(1)}, f32[640,128]{1,0:T(8,128)S(1)}, u32[]{:S(2)}, u32[]{:S(2)}) %collective-permute-start.38) | collective-permute-done | bytes 327712 | tf_op jit(solution)/shard_map/ppermute | solution.py:44
  159.0 6.0 %collective-permute-done.34.crossed = f32[512,128]{1,0:T(8,128)S(1)} collective-permute-done((f32[512,128]{1,0:T(8,128)S(1)}, f32[512,128]{1,0:T(8,128)S(1)}, u32[]{:S(2)}, u32[]{:S(2)}) %collective-permute-start.34) | collective-permute-done | bytes 262176 | tf_op jit(solution)/shard_map/ppermute | solution.py:429
  185.2 4.2 %collective-permute-start.52 = (f32[1536,128]{1,0:T(8,128)S(1)}, f32[1536,128]{1,0:T(8,128)S(1)}, u32[]{:S(2)}, u32[]{:S(2)}) collective-permute-start(f32[1536,128]{1,0:T(8,128)S(1)} %shard_map.114), channel_id=1, source_target_pairs={{0,4},{1,5},{2,6},{3,7},{4,0},{5,1},{6,2},{7,3},{8,12},{9,13},{10,... | collective-permute-start | bytes 2359304 | tf_op jit(solution)/shard_map/ppermute | solution.py:39
  190.8 5.0 %collective-permute-done.44.straight.refs_9_ = f32[640,128]{1,0:T(8,128)S(1)} collective-permute-done((f32[640,128]{1,0:T(8,128)S(1)}, f32[640,128]{1,0:T(8,128)S(1)}, u32[]{:S(2)}, u32[]{:S(2)}) %collective-permute-start.44) | collective-permute-done | bytes 327712 | tf_op jit(solution)/shard_map/ppermute | solution.py:429
  196.8 4.5 %collective-permute-start.53 = (f32[512,128]{1,0:T(8,128)S(1)}, f32[512,128]{1,0:T(8,128)S(1)}, u32[]{:S(2)}, u32[]{:S(2)}) collective-permute-start(f32[512,128]{1,0:T(8,128)S(1)} %collective-permute-done.49.refs_1_), channel_id=1, source_target_pairs={{0,4},{1,5},{2,6},{3,7},{4,0},{5,1},{6,2},{7,3},{8,12},{9,13},{10,... | collective-permute-start | bytes 786440 | tf_op jit(solution)/shard_map/ppermute | solution.py:39
  214.7 6.3 %collective-permute-done.62.refs_1_.refs_3_ = f32[512,128]{1,0:T(8,128)S(1)} collective-permute-done((f32[512,128]{1,0:T(8,128)S(1)}, f32[512,128]{1,0:T(8,128)S(1)}, u32[]{:S(2)}, u32[]{:S(2)}) %collective-permute-start.62) | collective-permute-done | bytes 262176 | tf_op jit(solution)/shard_map/ppermute | solution.py:44
  221.1 9.6 %collective-permute-start.63 = (f32[1536,128]{1,0:T(8,128)S(1)}, f32[1536,128]{1,0:T(8,128)S(1)}, u32[]{:S(2)}, u32[]{:S(2)}) collective-permute-start(f32[1536,128]{1,0:T(8,128)S(1)} %shard_map.118), channel_id=1, source_target_pairs={{0,4},{1,5},{2,6},{3,7},{4,0},{5,1},{6,2},{7,3},{8,12},{9,13},{10,... | collective-permute-start | bytes 2359304 | tf_op jit(solution)/shard_map/ppermute | solution.py:39
  232.2 4.8 %collective-permute-done.55.straight = f32[512,128]{1,0:T(8,128)S(1)} collective-permute-done((f32[512,128]{1,0:T(8,128)S(1)}, f32[512,128]{1,0:T(8,128)S(1)}, u32[]{:S(2)}, u32[]{:S(2)}) %collective-permute-start.55) | collective-permute-done | bytes 262176 | tf_op jit(solution)/shard_map/ppermute | solution.py:429
  240.7 5.1 %factor.2.inverse.first = f32[128,128]{1,0:T(8,128)S(1)} custom-call(f32[128,128]{1,0:T(8,128)S(1)} %get-tuple-element.81.gram), custom_call_target="tpu_custom_call" | custom-call | tf_op jit(solution)/shard_map/factor/pallas_call | solution.py:400
  261.8 5.7 %collective-permute-done.73.two.refs_1_.refs_3_ = f32[640,128]{1,0:T(8,128)S(1)} collective-permute-done((f32[640,128]{1,0:T(8,128)S(1)}, f32[640,128]{1,0:T(8,128)S(1)}, u32[]{:S(2)}, u32[]{:S(2)}) %collective-permute-start.73) | collective-permute-done | bytes 327712 | tf_op jit(solution)/shard_map/ppermute | solution.py:44
  268.1 5.0 %collective-permute-start.74 = (f32[1536,128]{1,0:T(8,128)S(1)}, f32[1536,128]{1,0:T(8,128)S(1)}, u32[]{:S(2)}, u32[]{:S(2)}) collective-permute-start(f32[1536,128]{1,0:T(8,128)S(1)} %shard_map.124), channel_id=1, source_target_pairs={{0,4},{1,5},{2,6},{3,7},{4,0},{5,1},{6,2},{7,3},{8,12},{9,13},{10,... | collective-permute-start | bytes 2359304 | tf_op jit(solution)/shard_map/ppermute | solution.py:39
  275.2 5.3 %collective-permute-done.71.one = f32[640,128]{1,0:T(8,128)S(1)} collective-permute-done((f32[640,128]{1,0:T(8,128)S(1)}, f32[640,128]{1,0:T(8,128)S(1)}, u32[]{:S(2)}, u32[]{:S(2)}) %collective-permute-start.71) | collective-permute-done | bytes 327712 | tf_op jit(solution)/shard_map/ppermute | solution.py:44
  298.3 4.9 %collective-permute-done.78 = f32[256,128]{1,0:T(8,128)S(1)} collective-permute-done((f32[256,128]{1,0:T(8,128)S(1)}, f32[256,128]{1,0:T(8,128)S(1)}, u32[]{:S(2)}, u32[]{:S(2)}) %collective-permute-start.78) | collective-permute-done | bytes 131104 | tf_op jit(solution)/shard_map/ppermute | solution.py:39
  316.4 5.1 %factor.3.inverse.second = f32[128,128]{1,0:T(8,128)S(1)} custom-call(f32[128,128]{1,0:T(8,128)S(1)} %get-tuple-element.91.gram), custom_call_target="tpu_custom_call" | custom-call | tf_op jit(solution)/shard_map/factor/pallas_call | solution.py:400
  (195 shorter events, 185.7 us)
Async XLA Ops:
  21.2 22.0 %collective-permute-start.8 = (f32[1536,128]{1,0:T(8,128)S(1)}, f32[1536,128]{1,0:T(8,128)S(1)}, u32[]{:S(2)}, u32[]{:S(2)}) collective-permute-start(f32[1536,128]{1,0:T(8,128)S(1)} %shard_map.97), channel_id=1, source_target_pairs={{0,4},{1,5},{2,6},{3,7},{4,0},{5,1},{6,2},{7,3},{8,12},{9,13},{10,... | collective-permute-start | bytes 2359304 | tf_op jit(solution)/shard_map/ppermute | solution.py:39
  28.6 11.9 %collective-permute-start.1 = (f32[512,128]{1,0:T(8,128)S(1)}, f32[512,128]{1,0:T(8,128)}, u32[]{:S(2)}, u32[]{:S(2)}) collective-permute-start(f32[512,128]{1,0:T(8,128)S(1)} %get-tuple-element.49.head.refs_0_), channel_id=1, source_target_pairs={{0,3},{1,0},{2,1},{3,2},{4,5},{5,6},{6,7},{7,4},{8,11},{9,8},{10,9... | collective-permute-start | bytes 786440 | tf_op jit(solution)/shard_map/ppermute | solution.py:429
  33.0 10.2 %collective-permute-start.10 = (f32[512,128]{1,0:T(8,128)}, f32[512,128]{1,0:T(8,128)S(1)}, u32[]{:S(2)}, u32[]{:S(2)}) collective-permute-start(f32[512,128]{1,0:T(8,128)} %collective-permute-done.straight), channel_id=1, source_target_pairs={{0,1},{1,2},{2,3},{3,0},{4,7},{5,4},{6,5},{7,6},{8,9},{9,10},{10,1... | collective-permute-start | bytes 786440 | tf_op jit(solution)/shard_map/ppermute | solution.py:429
  61.5 16.2 %collective-permute-start.19 = (f32[1536,128]{1,0:T(8,128)S(1)}, f32[1536,128]{1,0:T(8,128)S(1)}, u32[]{:S(2)}, u32[]{:S(2)}) collective-permute-start(f32[1536,128]{1,0:T(8,128)S(1)} %shard_map.101), channel_id=1, source_target_pairs={{0,4},{1,5},{2,6},{3,7},{4,0},{5,1},{6,2},{7,3},{8,12},{9,13},{10,... | collective-permute-start | bytes 2359304 | tf_op jit(solution)/shard_map/ppermute | solution.py:39
  66.1 9.9 %collective-permute-start.12 = (f32[512,128]{1,0:T(8,128)S(1)}, f32[512,128]{1,0:T(8,128)S(1)}, u32[]{:S(2)}, u32[]{:S(2)}) collective-permute-start(f32[512,128]{1,0:T(8,128)S(1)} %get-tuple-element.54.head.refs_0_), channel_id=1, source_target_pairs={{0,3},{1,0},{2,1},{3,2},{4,5},{5,6},{6,7},{7,4},{8,11},{9,8},{10,9... | collective-permute-start | bytes 786440 | tf_op jit(solution)/shard_map/ppermute | solution.py:429
  95.6 21.4 %collective-permute-start.30 = (f32[1536,128]{1,0:T(8,128)S(1)}, f32[1536,128]{1,0:T(8,128)S(1)}, u32[]{:S(2)}, u32[]{:S(2)}) collective-permute-start(f32[1536,128]{1,0:T(8,128)S(1)} %shard_map.105), channel_id=1, source_target_pairs={{0,4},{1,5},{2,6},{3,7},{4,0},{5,1},{6,2},{7,3},{8,12},{9,13},{10,... | collective-permute-start | bytes 2359304 | tf_op jit(solution)/shard_map/ppermute | solution.py:39
  105.3 9.9 %collective-permute-start.23 = (f32[512,128]{1,0:T(8,128)S(1)}, f32[512,128]{1,0:T(8,128)S(1)}, u32[]{:S(2)}, u32[]{:S(2)}) collective-permute-start(f32[512,128]{1,0:T(8,128)S(1)} %get-tuple-element.59.head), channel_id=1, source_target_pairs={{0,3},{1,0},{2,1},{3,2},{4,5},{5,6},{6,7},{7,4},{8,11},{9,8},{10,9... | collective-permute-start | bytes 786440 | tf_op jit(solution)/shard_map/ppermute | solution.py:429
  128.8 9.3 %collective-permute-start.39 = (f32[640,128]{1,0:T(8,128)S(1)}, f32[640,128]{1,0:T(8,128)S(1)}, u32[]{:S(2)}, u32[]{:S(2)}) collective-permute-start(f32[640,128]{1,0:T(8,128)S(1)} %shard_map.108.packed.refs_0_), channel_id=1, source_target_pairs={{0,96},{1,97},{2,98},{3,99},{4,28},{5,29},{6,30},{7,31},{8,104},{9... | collective-permute-start | bytes 983048 | tf_op jit(solution)/shard_map/ppermute | solution.py:44
  138.2 28.4 %collective-permute-start.41 = (f32[1536,128]{1,0:T(8,128)S(1)}, f32[1536,128]{1,0:T(8,128)S(1)}, u32[]{:S(2)}, u32[]{:S(2)}) collective-permute-start(f32[1536,128]{1,0:T(8,128)S(1)} %shard_map.110), channel_id=1, source_target_pairs={{0,4},{1,5},{2,6},{3,7},{4,0},{5,1},{6,2},{7,3},{8,12},{9,13},{10,... | collective-permute-start | bytes 2359304 | tf_op jit(solution)/shard_map/ppermute | solution.py:39
  155.6 11.0 %collective-permute-start.42 = (f32[640,128]{1,0:T(8,128)S(1)}, f32[640,128]{1,0:T(8,128)S(1)}, u32[]{:S(2)}, u32[]{:S(2)}) collective-permute-start(f32[640,128]{1,0:T(8,128)S(1)} %shard_map.109.refs_1_), channel_id=1, source_target_pairs={{0,4},{1,5},{2,6},{3,7},{4,0},{5,1},{6,2},{7,3},{8,12},{9,13},{10,... | collective-permute-start | bytes 983048 | tf_op jit(solution)/shard_map/ppermute | solution.py:39
  156.4 8.7 %collective-permute-start.34 = (f32[512,128]{1,0:T(8,128)S(1)}, f32[512,128]{1,0:T(8,128)S(1)}, u32[]{:S(2)}, u32[]{:S(2)}) collective-permute-start(f32[512,128]{1,0:T(8,128)S(1)} %get-tuple-element.64.head.refs_0_), channel_id=1, source_target_pairs={{0,3},{1,0},{2,1},{3,2},{4,5},{5,6},{6,7},{7,4},{8,11},{9,8},{10,9... | collective-permute-start | bytes 786440 | tf_op jit(solution)/shard_map/ppermute | solution.py:429
  157.1 9.5 %collective-permute-start.43 = (f32[512,128]{1,0:T(8,128)S(1)}, f32[512,128]{1,0:T(8,128)S(1)}, u32[]{:S(2)}, u32[]{:S(2)}) collective-permute-start(f32[512,128]{1,0:T(8,128)S(1)} %collective-permute-done.33.straight), channel_id=1, source_target_pairs={{0,1},{1,2},{2,3},{3,0},{4,7},{5,4},{6,5},{7,6},{8,9},{9,10},{10,1... | collective-permute-start | bytes 786440 | tf_op jit(solution)/shard_map/ppermute | solution.py:429
  176.6 8.5 %collective-permute-start.50 = (f32[512,128]{1,0:T(8,128)S(1)}, f32[512,128]{1,0:T(8,128)S(1)}, u32[]{:S(2)}, u32[]{:S(2)}) collective-permute-start(f32[512,128]{1,0:T(8,128)S(1)} %shard_map.113.refs_0_), channel_id=1, source_target_pairs={{0,96},{1,97},{2,98},{3,99},{4,28},{5,29},{6,30},{7,31},{8,104},{9... | collective-permute-start | bytes 786440 | tf_op jit(solution)/shard_map/ppermute | solution.py:44
  185.2 18.3 %collective-permute-start.52 = (f32[1536,128]{1,0:T(8,128)S(1)}, f32[1536,128]{1,0:T(8,128)S(1)}, u32[]{:S(2)}, u32[]{:S(2)}) collective-permute-start(f32[1536,128]{1,0:T(8,128)S(1)} %shard_map.114), channel_id=1, source_target_pairs={{0,4},{1,5},{2,6},{3,7},{4,0},{5,1},{6,2},{7,3},{8,12},{9,13},{10,... | collective-permute-start | bytes 2359304 | tf_op jit(solution)/shard_map/ppermute | solution.py:39
  189.4 11.9 %collective-permute-start.45 = (f32[640,128]{1,0:T(8,128)S(1)}, f32[640,128]{1,0:T(8,128)S(1)}, u32[]{:S(2)}, u32[]{:S(2)}) collective-permute-start(f32[640,128]{1,0:T(8,128)S(1)} %get-tuple-element.69.head.refs_8_.refs_0_), channel_id=1, source_target_pairs={{0,3},{1,0},{2,1},{3,2},{4,5},{5,6},{6,7},{7,4},{8,11},{9,8},{10,9... | collective-permute-start | bytes 983048 | tf_op jit(solution)/shard_map/ppermute | solution.py:429
  221.1 26.3 %collective-permute-start.63 = (f32[1536,128]{1,0:T(8,128)S(1)}, f32[1536,128]{1,0:T(8,128)S(1)}, u32[]{:S(2)}, u32[]{:S(2)}) collective-permute-start(f32[1536,128]{1,0:T(8,128)S(1)} %shard_map.118), channel_id=1, source_target_pairs={{0,4},{1,5},{2,6},{3,7},{4,0},{5,1},{6,2},{7,3},{8,12},{9,13},{10,... | collective-permute-start | bytes 2359304 | tf_op jit(solution)/shard_map/ppermute | solution.py:39
  230.7 15.1 %collective-permute-start.56 = (f32[512,128]{1,0:T(8,128)S(1)}, f32[512,128]{1,0:T(8,128)S(1)}, u32[]{:S(2)}, u32[]{:S(2)}) collective-permute-start(f32[512,128]{1,0:T(8,128)S(1)} %get-tuple-element.74.head), channel_id=1, source_target_pairs={{0,3},{1,0},{2,1},{3,2},{4,5},{5,6},{6,7},{7,4},{8,11},{9,8},{10,9... | collective-permute-start | bytes 786440 | tf_op jit(solution)/shard_map/ppermute | solution.py:429
  237.0 10.3 %collective-permute-start.65 = (f32[512,128]{1,0:T(8,128)S(1)}, f32[512,128]{1,0:T(8,128)S(1)}, u32[]{:S(2)}, u32[]{:S(2)}) collective-permute-start(f32[512,128]{1,0:T(8,128)S(1)} %collective-permute-done.55.straight), channel_id=1, source_target_pairs={{0,1},{1,2},{2,3},{3,0},{4,7},{5,4},{6,5},{7,6},{8,9},{9,10},{10,1... | collective-permute-start | bytes 786440 | tf_op jit(solution)/shard_map/ppermute | solution.py:429
  237.5 9.9 %collective-permute-start.64 = (f32[512,128]{1,0:T(8,128)S(1)}, f32[512,128]{1,0:T(8,128)S(1)}, u32[]{:S(2)}, u32[]{:S(2)}) collective-permute-start(f32[512,128]{1,0:T(8,128)S(1)} %collective-permute-done.60.refs_1_), channel_id=1, source_target_pairs={{0,4},{1,5},{2,6},{3,7},{4,0},{5,1},{6,2},{7,3},{8,12},{9,13},{10,... | collective-permute-start | bytes 786440 | tf_op jit(solution)/shard_map/ppermute | solution.py:39
  268.1 22.3 %collective-permute-start.74 = (f32[1536,128]{1,0:T(8,128)S(1)}, f32[1536,128]{1,0:T(8,128)S(1)}, u32[]{:S(2)}, u32[]{:S(2)}) collective-permute-start(f32[1536,128]{1,0:T(8,128)S(1)} %shard_map.124), channel_id=1, source_target_pairs={{0,4},{1,5},{2,6},{3,7},{4,0},{5,1},{6,2},{7,3},{8,12},{9,13},{10,... | collective-permute-start | bytes 2359304 | tf_op jit(solution)/shard_map/ppermute | solution.py:39
  273.1 8.5 %collective-permute-start.66 = (f32[512,128]{1,0:T(8,128)S(1)}, f32[512,128]{1,0:T(8,128)S(1)}, u32[]{:S(2)}, u32[]{:S(2)}) collective-permute-start(f32[512,128]{1,0:T(8,128)S(1)} %get-tuple-element.79.head), channel_id=1, source_target_pairs={{0,1},{1,2},{2,3},{3,0},{4,7},{5,4},{6,5},{7,6},{8,9},{9,10},{10,1... | collective-permute-start | bytes 786440 | tf_op jit(solution)/shard_map/ppermute | solution.py:429
  280.6 9.8 %collective-permute-start.75 = (f32[640,128]{1,0:T(8,128)S(1)}, f32[640,128]{1,0:T(8,128)S(1)}, u32[]{:S(2)}, u32[]{:S(2)}) collective-permute-start(f32[640,128]{1,0:T(8,128)S(1)} %shard_map.123.refs_1_), channel_id=1, source_target_pairs={{0,4},{1,5},{2,6},{3,7},{4,0},{5,1},{6,2},{7,3},{8,12},{9,13},{10,... | collective-permute-start | bytes 983048 | tf_op jit(solution)/shard_map/ppermute | solution.py:39
  281.6 8.8 %collective-permute-start.76 = (f32[512,128]{1,0:T(8,128)S(1)}, f32[512,128]{1,0:T(8,128)S(1)}, u32[]{:S(2)}, u32[]{:S(2)}) collective-permute-start(f32[512,128]{1,0:T(8,128)S(1)} %collective-permute-done.66.straight), channel_id=1, source_target_pairs={{0,1},{1,2},{2,3},{3,0},{4,7},{5,4},{6,5},{7,6},{8,9},{9,10},{10,1... | collective-permute-start | bytes 786440 | tf_op jit(solution)/shard_map/ppermute | solution.py:429
  313.5 9.6 %collective-permute-start.86 = (f32[128,128]{1,0:T(8,128)S(1)}, f32[128,128]{1,0:T(8,128)S(1)}, u32[]{:S(2)}, u32[]{:S(2)}) collective-permute-start(f32[128,128]{1,0:T(8,128)S(1)} %add_add_fusion.2), channel_id=1, source_target_pairs={{0,96},{1,97},{2,98},{3,99},{4,100},{5,101},{6,102},{7,103},{8,104... | collective-permute-start | bytes 196616 | tf_op jit(solution)/shard_map/ppermute | solution.py:39
  (64 other events, 380.3 us)
